TPU v7x, 256 devices: a whole 4x4x8 slice. The times are simulated.
256 devices in a mesh: dom: 64 (over y, z, core), rep: 4 (over x).
Axes of the slice: x: 4, y: 4, z: 8, core: 2. Of those that a mesh axis runs over, the one named last changes fastest.
Arguments:
- inflow_pressure: float32 [32, 262144], P('rep', 'dom'), may hold values from -6 to 6
- inflow_mask: int32 [262144], P('dom'), may hold values 0 or 1
- seg_ends: int32 [2, 458752], P(None, 'dom'), may hold values from 0 to 4095, as said below
- live_counts: int32 [64], P('dom'), may hold values from 3072 to 6144, as said below
- shown_blocks: int32 [512], P('dom'), may hold values from 0 to 31, as said below
- radius: float32 [458752], P('dom'), may hold values from 3 to 6
- seg_length: float32 [458752], P('dom'), may hold values from 20 to 100
Outputs:
- pressure: float32 [32, 262144], P('rep', 'dom')
- mean_pressure: float32 [262144], P('dom')
Inputs may be any that keep to these rules, and one draw needn't show every extreme that they name: `seg_ends`: row 0 holds local node ids; for inner slots row 1 holds a local node id different from row 0, for junction slots a slot of the upper partition below 1024. `live_counts`: some partition has all inner slots live. `shown_blocks`: distinct within each partition.
All inputs are finite; a program needn't handle non-finite values. No bound on the sum of `inflow_mask` on one device may be relied on, other than what follows from the above.
Results may differ from a plain program's by a relative error of at most 0.0018.
Values may be sent and summed in bfloat16 or wider, within the bound.
A program may use at most 64 MiB of HBM per device.

v0:
```python
import math

import jax
import jax.numpy as jnp
from jax import lax
from jax.sharding import PartitionSpec as P

TILE_NODES = 128
SCENARIOS = 32
ITERATIONS = 3
JUNCTIONS = 1024
INNER_SEGS = 6144
SEGS_DEV = 7168


leak_rate = 0.05
inflow_weight = 20.0


def passed_along(value, axis, steps):
    count = lax.axis_size(axis)
    initial, last = (max(0, -steps), min(count, count - steps))
    return lax.ppermute(value, axis, [(source, source + steps) for source in range(initial, last)])


def conductance(radius, seg_length):
    diameter = 2.0 * radius
    viscous = 220.0 * jnp.exp(-1.3 * diameter) + 3.2 - 2.44 * jnp.exp(-0.06 * diameter**0.645)
    return (diameter / 8.0) ** 4 * (50.0 / seg_length) / viscous


def block_inverses(head, tail, weight, degree, first, count):
    group = math.gcd(count, 32)
    same = head // TILE_NODES == tail // TILE_NODES
    weight = jnp.where(same, weight, 0.0)
    row = head % TILE_NODES
    column = tail % TILE_NODES
    owner = head // TILE_NODES
    diag_tiles = degree.reshape(-1, TILE_NODES)
    unit = jnp.eye(TILE_NODES, dtype=jnp.float32)

    def one_group(start):
        local = owner - start
        inside = (local >= 0) & (local < group)
        safe = jnp.where(inside, local, 0)
        taken = jnp.where(inside, weight, 0.0)
        flat_one = (safe * TILE_NODES + row) * TILE_NODES + column
        flat_two = (safe * TILE_NODES + column) * TILE_NODES + row
        tiles = jnp.zeros(group * TILE_NODES * TILE_NODES, jnp.float32)
        tiles = tiles.at[flat_one].add(-taken).at[flat_two].add(-taken)
        tiles = tiles.reshape(group, TILE_NODES, TILE_NODES)
        tiles = tiles + diag_tiles[:, :, None] * unit
        factor = jnp.linalg.cholesky(tiles)
        inverse = jax.scipy.linalg.cho_solve((factor, True), jnp.broadcast_to(unit, tiles.shape))
        return inverse.astype(jnp.bfloat16)

    starts = first + jnp.arange(count // group, dtype=jnp.int32) * group
    return lax.map(one_group, starts).reshape(count, TILE_NODES, TILE_NODES)


def per_device(
    inflow_pressure, inflow_mask, seg_ends, live_counts, shown_blocks, radius, seg_length
):
    scen, nodes = inflow_pressure.shape
    blocks = nodes // TILE_NODES
    parts = lax.axis_size("dom")
    place = lax.axis_index("dom")
    cond = conductance(radius, seg_length)
    position = jnp.arange(SEGS_DEV, dtype=jnp.int32)
    live = jnp.where(position < INNER_SEGS, position < live_counts[0], place < parts - 1)
    cond = jnp.where(live, cond, 0.0)
    inner_head = seg_ends[0, :INNER_SEGS]
    inner_tail = seg_ends[1, :INNER_SEGS]
    inner_cond = cond[:INNER_SEGS]
    junc_head = seg_ends[0, INNER_SEGS:]
    junc_slot = seg_ends[1, INNER_SEGS:]
    junc_cond = cond[INNER_SEGS:]
    extra = leak_rate + inflow_weight * inflow_mask.astype(jnp.float32)
    slot_cond = jnp.zeros(JUNCTIONS, jnp.float32).at[junc_slot].add(junc_cond)
    arrived = passed_along(slot_cond, "dom", 1)
    degree = (
        jnp.zeros(nodes, jnp.float32).at[inner_head].add(inner_cond).at[inner_tail].add(inner_cond)
    )
    degree = degree.at[junc_head].add(junc_cond)
    degree = (
        degree.reshape(blocks, TILE_NODES)
        .at[shown_blocks]
        .add(arrived.reshape(-1, TILE_NODES))
        .reshape(nodes)
    )
    degree = degree + extra
    inverse = block_inverses(inner_head, inner_tail, inner_cond, degree, 0, blocks)
    upper_lists = passed_along(shown_blocks, "dom", -1)

    def precond(field):
        rounded = field.astype(jnp.bfloat16).reshape(scen, blocks, TILE_NODES)
        return jnp.einsum(
            "bij,sbj->sbi", inverse, rounded, preferred_element_type=jnp.float32
        ).reshape(scen, nodes)

    def residual_product(residual, z_field):
        return lax.psum(jnp.sum(residual * z_field, axis=1), "dom")

    rhs = inflow_weight * inflow_mask.astype(jnp.float32)[None, :] * inflow_pressure
    pressure = jnp.zeros_like(rhs)
    residual = rhs
    z_field = precond(residual)
    direction = z_field
    rz_now = residual_product(residual, z_field)
    for step in range(ITERATIONS):
        upper = passed_along(direction, "dom", -1)
        tiles = upper.reshape(scen, blocks, TILE_NODES)[:, upper_lists].reshape(scen, JUNCTIONS)
        inner_flow = inner_cond * (direction[:, inner_head] - direction[:, inner_tail])
        junc_flow = junc_cond * (direction[:, junc_head] - tiles[:, junc_slot])
        out = extra * direction
        out = (
            out.at[:, inner_head]
            .add(inner_flow)
            .at[:, inner_tail]
            .add(-inner_flow)
            .at[:, junc_head]
            .add(junc_flow)
        )
        back = jnp.zeros((scen, JUNCTIONS), jnp.float32).at[:, junc_slot].add(junc_flow)
        back = passed_along(back, "dom", 1)
        out = (
            out.reshape(scen, blocks, TILE_NODES)
            .at[:, shown_blocks]
            .add(-back.reshape(scen, -1, TILE_NODES))
        )
        image = out.reshape(scen, nodes)
        alpha = rz_now / lax.psum(jnp.sum(direction * image, axis=1), "dom")
        pressure = pressure + alpha[:, None] * direction
        residual = residual - alpha[:, None] * image
        if step + 1 < ITERATIONS:
            z_field = precond(residual)
            rz_next = residual_product(residual, z_field)
            direction = z_field + (rz_next / rz_now)[:, None] * direction
            rz_now = rz_next
    mean_pressure = lax.psum(jnp.sum(pressure, axis=0), "rep") / SCENARIOS
    return (pressure, mean_pressure)


def solution(mesh):
    in_specs = (P("rep", "dom"), P("dom"), P(None, "dom"), P("dom"), P("dom"), P("dom"), P("dom"))
    out_specs = (P("rep", "dom"), P("dom"))
    return jax.shard_map(
        per_device, mesh=mesh, in_specs=in_specs, out_specs=out_specs, check_vma=False
    )
```

profile of v0, /device:TPU:1, one launch (start us, length us, event | category | flops | bytes accessed | tf_op | source)
XLA Modules:
  0.0 2008.9 jit_solution(7489639887311938558)
XLA Ops:
  0.6 5.1 collective-permute-start.2
  8.0 7.6 scatter_custom_fusion.5
  20.8 32.6 %scatter_custom_fusion.2 = f32[4096]{0:T(1024)S(1)} fusion(s32[6144]{0:T(1024)S(1)} %bitcast.192, f32[6144]{0:T(1024)S(1)} %get-tuple-element.64, f32[]{:T(128)} %constant.143.clone.1), kind=kCustom, calls=%fused_computation.159 | custom fusion | flops 6144 | bytes 16388 | tf_op jit(solution)/shard_map/scatter-add | solution.py:82
  53.3 33.3 %scatter_fusion.1 = f32[4096]{0:T(1024)S(1)} fusion(f32[4096]{0:T(1024)S(1)} %scatter_custom_fusion.2, s32[6144]{0:T(1024)S(1)} %bitcast.179, f32[6144]{0:T(1024)S(1)} %get-tuple-element.64), kind=kCustom, calls=%fused_computation.18 | custom fusion | flops 6144 | bytes 98304 | tf_op jit(solution)/shard_map/scatter-add | solution.py:82
  86.7 6.1 scatter_fusion.2
  92.7 33.1 %scatter_custom_fusion = f32[524288]{0:T(1024)S(1)} fusion(s32[6144]{0:T(1024)S(1)} %bitcast.204, f32[6144]{0:T(1024)S(1)} %get-tuple-element.65, f32[]{:T(128)} %constant.143.clone.1), kind=kCustom, calls=%fused_computation.57 | custom fusion | flops 6144 | bytes 2097156 | tf_op jit(solution)/shard_map/while/body/eval_jaxpr/scatter-add | solution.py:50
  125.8 34.1 %scatter_fusion = f32[524288]{0:T(1024)S(1)} fusion(f32[524288]{0:T(1024)S(1)} %scatter_custom_fusion, s32[6144]{0:T(1024)S(1)} %bitcast.190, f32[6144]{0:T(1024)S(1)} %get-tuple-element.65), kind=kCustom, calls=%fused_computation.16 | custom fusion | flops 6144 | bytes 98304 | tf_op jit(solution)/shard_map/while/body/eval_jaxpr/scatter-add | solution.py:50
  162.7 3.3 multiply_add_fusion
  166.0 3.0 copy.244
  169.0 3.3 fusion.10
  172.3 375.8 %custom-call.13 = f32[32,128,128]{2,1,0:T(8,128)S(1)} custom-call(f32[32,128,128]{2,1,0:T(8,128)} %fusion.10), custom_call_target="Cholesky" | custom-call | tf_op jit(solution)/shard_map/while/body/eval_jaxpr/jit(cholesky)/cholesky | solution.py:53
  550.1 315.5 %custom-call.14 = f32[32,1,128,128]{2,3,1,0:T(8,128)S(1)} custom-call(f32[32,1,128,128]{3,2,1,0:T(8,128)} %select_bitcast_fusion), custom_call_target="InvertDiagBlocksLowerTriangular" | custom-call | tf_op jit(solution)/shard_map/while/body/eval_jaxpr/jit(_cho_solve)/vmap()/triangular_solve | solution.py:54
  865.5 3.5 fusion.8
  875.8 4.0 gather_fusion.2
  883.7 5.0 gather_fusion.4
  888.8 7.9 scatter_custom_fusion.10
  896.6 3.1 collective-permute-start.3
  901.8 20.9 %gather_fusion.1 = f32[6144,8]{1,0:T(8,128)} fusion(f32[8,4096]{0,1:T(8,128)S(1)} %copy.247, s32[6144]{0:T(1024)S(1)} %broadcast_clamp_fusion), kind=kCustom, calls=%fused_computation.1 | custom fusion | bytes 417792 | tf_op jit(solution)/shard_map/gather | solution.py:113
  922.6 20.9 %gather_fusion = f32[6144,8]{1,0:T(8,128)} fusion(f32[8,4096]{0,1:T(8,128)S(1)} %copy.247, s32[6144]{0:T(1024)S(1)} %broadcast_clamp_fusion.1), kind=kCustom, calls=%fused_computation | custom fusion | bytes 417792 | tf_op jit(solution)/shard_map/gather | solution.py:113
  943.5 39.7 %scatter_custom_fusion.7 = f32[8,4096]{0,1:T(8,128)} fusion(f32[8,4096]{0,1:T(8,128)} %copy.249, s32[6144]{0:T(1024)} %bitcast.193, f32[6144,8]{1,0:T(8,128)} %gather_fusion, f32[6144,8]{1,0:T(8,128)} %gather_fusion.1, f32[6144]{0:T(1024)S(1)} %get-tuple-element.64), kind=kCustom, calls=%fused_computation.62 | custom fusion | flops 147456 | bytes 6447104 | tf_op jit(solution)/shard_map/scatter-add | solution.py:118
  983.3 39.7 %scatter_custom_fusion.8 = f32[8,4096]{0,1:T(8,128)} fusion(f32[8,4096]{0,1:T(8,128)} %scatter_custom_fusion.7, s32[6144]{0:T(1024)S(1)} %bitcast.181, f32[6144,8]{1,0:T(8,128)} %gather_fusion, f32[6144,8]{1,0:T(8,128)} %gather_fusion.1, f32[6144]{0:T(1024)S(1)} %get-tuple-element.64), kind=kCustom, calls=%fused_computation.41 | custom fusion | flops 196608 | bytes 6447104 | tf_op jit(solution)/shard_map/scatter-add | solution.py:120
  1023.0 9.4 scatter_custom_fusion.9
  1036.8 125.5 %all-reduce = (f32[8]{0:T(128)S(1)}, f32[8]{0:T(128)S(1)}) all-reduce(f32[8]{0:T(128)S(1)} %get-tuple-element.52, f32[8]{0:T(128)S(1)} %fusion.33), channel_id=1, replica_groups=mesh['dom'=64,'rep'=4] {'dom'}, use_global_device_ids=true, to_apply=%region_10.11 | all-reduce | flops 16 | bytes 128 | tf_op jit(solution)/shard_map/psum | solution.py:102
  1163.7 128.0 %psum.51 = f32[8]{0:T(128)S(1)} all-reduce(f32[8]{0:T(128)S(1)} %get-tuple-element.70), channel_id=1, replica_groups=mesh['dom'=64,'rep'=4] {'dom'}, use_global_device_ids=true, to_apply=%region_19.20 | all-reduce | flops 8 | bytes 64 | tf_op jit(solution)/shard_map/psum | solution.py:102
  1293.0 2.5 collective-permute-start.4
  1296.2 4.0 gather_fusion.7
  1304.1 5.0 gather_fusion.9
  1309.1 7.8 scatter_custom_fusion.15
  1316.9 3.0 collective-permute-start.5
  1319.9 22.9 %gather_fusion.6 = f32[6144,8]{1,0:T(8,128)} fusion(f32[8,4096]{0,1:T(8,128)S(1)} %copy.254, s32[6144]{0:T(1024)} %copy-done.16), kind=kCustom, calls=%fused_computation.6 | custom fusion | bytes 417792 | tf_op jit(solution)/shard_map/gather | solution.py:113
  1342.8 22.9 %gather_fusion.5 = f32[6144,8]{1,0:T(8,128)} fusion(f32[8,4096]{0,1:T(8,128)S(1)} %copy.254, s32[6144]{0:T(1024)} %copy-done.15), kind=kCustom, calls=%fused_computation.5 | custom fusion | bytes 417792 | tf_op jit(solution)/shard_map/gather | solution.py:113
  1367.2 37.3 %scatter_custom_fusion.12 = f32[8,4096]{0,1:T(8,128)S(1)} fusion(f32[8,4096]{0,1:T(8,128)S(1)} %copy.256, s32[6144]{0:T(1024)} %bitcast.194, f32[6144,8]{1,0:T(8,128)} %gather_fusion.5, f32[6144,8]{1,0:T(8,128)} %gather_fusion.6, f32[6144]{0:T(1024)} %copy-done.8), kind=kCustom, calls=%fused_computation.63 | custom fusion | flops 147456 | bytes 6447104 | tf_op jit(solution)/shard_map/scatter-add | solution.py:118
  1404.5 37.5 %scatter_custom_fusion.13 = f32[8,4096]{0,1:T(8,128)S(1)} fusion(f32[8,4096]{0,1:T(8,128)S(1)} %scatter_custom_fusion.12, s32[6144]{0:T(1024)} %bitcast.182, f32[6144,8]{1,0:T(8,128)} %gather_fusion.5, f32[6144,8]{1,0:T(8,128)} %gather_fusion.6, f32[6144]{0:T(1024)} %copy-done.8), kind=kCustom, calls=%fused_computation.39 | custom fusion | flops 196608 | bytes 6447104 | tf_op jit(solution)/shard_map/scatter-add | solution.py:120
  1442.0 7.2 scatter_custom_fusion.14
  1455.1 123.6 %psum.52 = f32[8]{0:T(128)S(1)} all-reduce(f32[8]{0:T(128)S(1)} %multiply_reduce_fusion.1), channel_id=1, replica_groups=mesh['dom'=64,'rep'=4] {'dom'}, use_global_device_ids=true, to_apply=%region_26.27 | all-reduce | flops 8 | bytes 64 | tf_op jit(solution)/shard_map/psum | solution.py:132
  1580.5 124.3 %psum.53 = f32[8]{0:T(128)S(1)} all-reduce(f32[8]{0:T(128)S(1)} %get-tuple-element.72), channel_id=1, replica_groups=mesh['dom'=64,'rep'=4] {'dom'}, use_global_device_ids=true, to_apply=%region_28.29 | all-reduce | flops 8 | bytes 64 | tf_op jit(solution)/shard_map/psum | solution.py:102
  1708.8 2.8 gather_fusion.12
  1713.6 3.8 gather_fusion.14
  1717.4 7.5 scatter_custom_fusion.20
  1725.0 2.7 collective-permute-start.7
  1727.7 22.9 %gather_fusion.11 = f32[6144,8]{1,0:T(8,128)} fusion(f32[8,4096]{0,1:T(8,128)S(1)} %copy.261, s32[6144]{0:T(1024)} %copy-done.16), kind=kCustom, calls=%fused_computation.11 | custom fusion | bytes 417792 | tf_op jit(solution)/shard_map/gather | solution.py:113
  1750.6 22.9 %gather_fusion.10 = f32[6144,8]{1,0:T(8,128)} fusion(f32[8,4096]{0,1:T(8,128)S(1)} %copy.261, s32[6144]{0:T(1024)} %copy-done.15), kind=kCustom, calls=%fused_computation.10 | custom fusion | bytes 417792 | tf_op jit(solution)/shard_map/gather | solution.py:113
  1773.5 2.9 copy.263
  1776.4 39.8 %scatter_custom_fusion.17 = f32[8,4096]{0,1:T(8,128)} fusion(f32[8,4096]{0,1:T(8,128)} %copy.263, s32[6144]{0:T(1024)} %bitcast.195, f32[6144,8]{1,0:T(8,128)} %gather_fusion.10, f32[6144,8]{1,0:T(8,128)} %gather_fusion.11, f32[6144]{0:T(1024)} %copy-done.8), kind=kCustom, calls=%fused_computation.64 | custom fusion | flops 147456 | bytes 6447104 | tf_op jit(solution)/shard_map/scatter-add | solution.py:118
  1816.2 39.3 %scatter_custom_fusion.18 = f32[8,4096]{0,1:T(8,128)} fusion(f32[8,4096]{0,1:T(8,128)} %scatter_custom_fusion.17, s32[6144]{0:T(1024)} %bitcast.183, f32[6144,8]{1,0:T(8,128)} %gather_fusion.10, f32[6144,8]{1,0:T(8,128)S(1)} %copy-done.1, f32[6144]{0:T(1024)} %copy-done.8), kind=kCustom, calls=%fused_computation.37 | custom fusion | flops 196608 | bytes 3497984 | tf_op jit(solution)/shard_map/scatter-add | solution.py:120
  1855.5 9.9 scatter_custom_fusion.19
  1869.9 123.8 %psum.54 = f32[8]{0:T(128)S(1)} all-reduce(f32[8]{0:T(128)S(1)} %multiply_reduce_fusion), channel_id=1, replica_groups=mesh['dom'=64,'rep'=4] {'dom'}, use_global_device_ids=true, to_apply=%region_35.36 | all-reduce | flops 8 | bytes 64 | tf_op jit(solution)/shard_map/psum | solution.py:132
  1994.7 13.1 psum.55
  (156 shorter events, 56.5 us)
Async XLA Ops:
  0.6 873.9 %collective-permute-start.2 = (s32[8]{0:T(128)}, s32[8]{0:T(128)}, u32[]{:S(2)}, u32[]{:S(2)}) collective-permute-start(s32[8]{0:T(128)} %param.11), channel_id=1, source_target_pairs={{4,0},{8,4},{12,8},{16,12},{20,16},{24,20},{28,24},{32,28},{36,32}... | collective-permute-start | bytes 104 | tf_op jit(solution)/shard_map/ppermute | solution.py:23
  7.2 79.5 %copy-start.23 = (s32[1024,1]{0,1:T(1,128)}, s32[1024,1]{0,1:T(1,128)S(1)}, u32[]{:S(2)}) copy-start(s32[1024,1]{0,1:T(1,128)S(1)} %get-tuple-element.54) | copy-start | bytes 12292
  15.7 146.1 %collective-permute-start = (f32[1024]{0:T(1024)S(1)}, f32[1024]{0:T(1024)S(1)}, u32[]{:S(2)}, u32[]{:S(2)}) collective-permute-start(f32[1024]{0:T(1024)S(1)} %scatter_custom_fusion.5), channel_id=1, source_target_pairs={{0,4},{4,8},{8,12},{12,16},{16,20},{20,24},{24,28},{28,32},{32,36}... | collective-permute-start | bytes 12296 | tf_op jit(solution)/shard_map/ppermute | solution.py:23
  18.2 143.6 %copy-start.29 = (s32[8]{0:T(128)}, s32[8]{0:T(128)S(1)}, u32[]{:S(2)}) copy-start(s32[8]{0:T(128)S(1)} %compare_select_fusion.12) | copy-start | bytes 100
  20.4 66.2 %copy-start.21 = (s32[6144,1]{0,1:T(1,128)}, s32[6144,1]{0,1:T(1,128)S(1)}, u32[]{:S(2)}) copy-start(s32[6144,1]{0,1:T(1,128)S(1)} %get-tuple-element.57) | copy-start | bytes 73732
  20.5 962.8 %copy-start.20 = (s32[6144,1]{0,1:T(1,128)}, s32[6144,1]{0,1:T(1,128)S(1)}, u32[]{:S(2)}) copy-start(s32[6144,1]{0,1:T(1,128)S(1)} %get-tuple-element.56) | copy-start | bytes 73732
  20.5 902.1 %copy-start.15 = (s32[6144]{0:T(1024)}, s32[6144]{0:T(1024)S(1)}, u32[]{:S(2)}) copy-start(s32[6144]{0:T(1024)S(1)} %broadcast_clamp_fusion.1) | copy-start | bytes 73732
  20.5 962.7 %copy-start.8 = (f32[6144]{0:T(1024)}, f32[6144]{0:T(1024)S(1)}, u32[]{:S(2)}) copy-start(f32[6144]{0:T(1024)S(1)} %get-tuple-element.64) | copy-start | bytes 73732
  159.9 2.7 copy-start.22
  162.7 708.6 %copy-start.17 = (f32[4096]{0:T(1024)}, f32[4096]{0:T(1024)S(1)}, u32[]{:S(2)}) copy-start(f32[4096]{0:T(1024)S(1)} %get-tuple-element.67) | copy-start | bytes 49156
  166.0 3.0 copy-start
  869.0 2.3 copy-start.13
  872.1 7.7 collective-permute-start.1
  875.2 21.4 %copy-start.26 = (s32[1024]{0:T(1024)}, s32[1024]{0:T(1024)S(1)}, u32[]{:S(2)}) copy-start(s32[1024]{0:T(1024)S(1)} %pad_clamp_fusion) | copy-start | bytes 12292
  896.6 138.0 %collective-permute-start.3 = (f32[8,1024]{0,1:T(8,128)}, f32[8,1024]{0,1:T(8,128)}, u32[]{:S(2)}, u32[]{:S(2)}) collective-permute-start(f32[8,1024]{0,1:T(8,128)} %scatter_custom_fusion.10), channel_id=1, source_target_pairs={{0,4},{4,8},{8,12},{12,16},{16,20},{20,24},{24,28},{28,32},{32,36}... | collective-permute-start | bytes 98312 | tf_op jit(solution)/shard_map/ppermute | solution.py:23
  899.8 43.7 %copy-start.16 = (s32[6144]{0:T(1024)}, s32[6144]{0:T(1024)S(1)}, u32[]{:S(2)}) copy-start(s32[6144]{0:T(1024)S(1)} %broadcast_clamp_fusion) | copy-start | bytes 73732
  983.3 39.7 %copy-start.4 = (f32[1024,8]{1,0:T(8,128)S(1)}, f32[1024,8]{1,0:T(8,128)}, u32[]{:S(2)}) copy-start(f32[1024,8]{1,0:T(8,128)} %gather_fusion.2) | copy-start | bytes 98308
  983.3 39.7 %copy-start.5 = (f32[1024,8]{1,0:T(8,128)S(1)}, f32[1024,8]{1,0:T(8,128)}, u32[]{:S(2)}) copy-start(f32[1024,8]{1,0:T(8,128)} %gather_fusion.4) | copy-start | bytes 98308
  1032.4 3.5 copy-start.30
  1032.4 130.4 %copy-start.14 = (f32[8,4096]{1,0:T(8,128)S(1)}, f32[8,4096]{1,0:T(8,128)}, u32[]{:S(2)}) copy-start(f32[8,4096]{1,0:T(8,128)} %param.7) | copy-start | bytes 393220
  1034.6 257.6 %copy-start.18 = (f32[4096]{0:T(1024)S(1)}, f32[4096]{0:T(1024)}, u32[]{:S(2)}) copy-start(f32[4096]{0:T(1024)} %copy-done.17) | copy-start | bytes 49156
  1162.4 0.5 copy-start.32
  1162.9 130.1 %copy-start.11 = (f32[8,4096]{1,0:T(8,128)}, f32[8,4096]{1,0:T(8,128)S(1)}, u32[]{:S(2)}) copy-start(f32[8,4096]{1,0:T(8,128)S(1)} %fusion.29) | copy-start | bytes 393220
  1291.7 0.6 copy-start.38
  1292.2 0.8 copy-start.24
  1293.0 7.1 collective-permute-start.4
  1316.9 133.6 %collective-permute-start.5 = (f32[8,1024]{0,1:T(8,128)}, f32[8,1024]{0,1:T(8,128)}, u32[]{:S(2)}, u32[]{:S(2)}) collective-permute-start(f32[8,1024]{0,1:T(8,128)} %scatter_custom_fusion.15), channel_id=1, source_target_pairs={{0,4},{4,8},{8,12},{12,16},{16,20},{20,24},{24,28},{28,32},{32,36}... | collective-permute-start | bytes 98312 | tf_op jit(solution)/shard_map/ppermute | solution.py:23
  1450.5 128.2 %copy-start.39 = (f32[8]{0:T(128)S(1)}, f32[8]{0:T(128)}, u32[]{:S(2)}) copy-start(f32[8]{0:T(128)} %copy-done.38) | copy-start | bytes 100
  1450.5 128.2 %copy-start.12 = (f32[8,4096]{1,0:T(8,128)S(1)}, f32[8,4096]{1,0:T(8,128)}, u32[]{:S(2)}) copy-start(f32[8,4096]{1,0:T(8,128)} %copy-done.11) | copy-start | bytes 393220
  1450.5 254.4 %copy-start.19 = (f32[4096]{0:T(1024)S(1)}, f32[4096]{0:T(1024)}, u32[]{:S(2)}) copy-start(f32[4096]{0:T(1024)} %copy-done.17) | copy-start | bytes 49156
  1578.7 130.1 %copy-start.27 = (f32[8]{0:T(128)}, f32[8]{0:T(128)S(1)}, u32[]{:S(2)}) copy-start(f32[8]{0:T(128)S(1)} %div.96) | copy-start | bytes 100
  1580.5 125.1 %copy-start.6 = (f32[32,8,128]{2,1,0:T(8,128)}, f32[32,8,128]{2,1,0:T(8,128)S(1)}, u32[]{:S(2)}) copy-start(f32[32,8,128]{2,1,0:T(8,128)S(1)} %get-tuple-element.73) | copy-start | bytes 393220
  1704.8 7.0 copy-start.36
  1704.8 7.0 copy-start.34
  1705.6 7.0 copy-start.9
  1705.6 6.3 collective-permute-start.6
  1711.6 39.0 %copy-start.2 = (f32[1024,8]{1,0:T(8,128)}, f32[1024,8]{1,0:T(8,128)S(1)}, u32[]{:S(2)}) copy-start(f32[1024,8]{1,0:T(8,128)S(1)} %gather_fusion.12) | copy-start | bytes 98308
  1717.4 56.1 %copy-start.3 = (f32[1024,8]{1,0:T(8,128)}, f32[1024,8]{1,0:T(8,128)S(1)}, u32[]{:S(2)}) copy-start(f32[1024,8]{1,0:T(8,128)S(1)} %gather_fusion.14) | copy-start | bytes 98308
  1725.0 142.7 %collective-permute-start.7 = (f32[8,1024]{0,1:T(8,128)}, f32[8,1024]{0,1:T(8,128)}, u32[]{:S(2)}, u32[]{:S(2)}) collective-permute-start(f32[8,1024]{0,1:T(8,128)} %scatter_custom_fusion.20), channel_id=1, source_target_pairs={{0,4},{4,8},{8,12},{12,16},{16,20},{20,24},{24,28},{28,32},{32,36}... | collective-permute-start | bytes 98312 | tf_op jit(solution)/shard_map/ppermute | solution.py:23
  1776.3 39.8 %copy-start.1 = (f32[6144,8]{1,0:T(8,128)S(1)}, f32[6144,8]{1,0:T(8,128)}, u32[]{:S(2)}) copy-start(f32[6144,8]{1,0:T(8,128)} %gather_fusion.11) | copy-start | bytes 589828
  1865.4 3.5 copy-start.31
  1865.4 4.3 copy-start.7
  1865.4 4.3 copy-start.25
  1865.4 4.3 copy-start.35
  1865.4 128.4 %copy-start.37 = (f32[8]{0:T(128)S(1)}, f32[8]{0:T(128)}, u32[]{:S(2)}) copy-start(f32[8]{0:T(128)} %copy-done.36) | copy-start | bytes 100
  1865.4 128.4 %copy-start.28 = (f32[8]{0:T(128)S(1)}, f32[8]{0:T(128)}, u32[]{:S(2)}) copy-start(f32[8]{0:T(128)} %copy-done.27) | copy-start | bytes 100
  1865.4 128.4 %copy-start.33 = (f32[8]{0:T(128)S(1)}, f32[8]{0:T(128)}, u32[]{:S(2)}) copy-start(f32[8]{0:T(128)} %copy-done.32) | copy-start | bytes 100
  1865.4 128.5 %copy-start.10 = (f32[8,4096]{1,0:T(8,128)S(1)}, f32[8,4096]{1,0:T(8,128)}, u32[]{:S(2)}) copy-start(f32[8,4096]{1,0:T(8,128)} %copy-done.9) | copy-start | bytes 393220
where the time goes:
time: 2020 us; the launch traced here: 2010 us
  other arithmetic  1150 us (57%)
  blocking collectives  638 us (32%)
  local copies, waits for them, and re-layouts  189 us (9%)
  starting transfers between devices  23.4 us (1%)
    psum x3, blocking collectives, residual_product(): return lax.psum(jnp.sum(residual * z_field, axis=1), 'dom')  378 us
    another operation x4, other arithmetic, one_group(): factor = jnp.linalg.cholesky(tiles)  376 us
    another operation x3, other arithmetic, one_group(): jax.scipy.linalg.cho_solve((factor, True), jnp.broadcast_to(unit, tiles.s...  317 us
    scatter-add x9, other arithmetic, per_device(): out = out.at[:, inner_head].add(inner_flow).at[:, inner_tail].add(-inner_...  260 us
    psum x2, blocking collectives, per_device(): alpha = rz_now / lax.psum(jnp.sum(direction * image, axis=1), 'dom')  247 us
    scatter-add x2, other arithmetic, one_group(): tiles = tiles.at[flat_one].add(-taken).at[flat_two].add(-taken)  67.2 us
    gather x3, local copies, waits for them, and re-layouts, per_device(): direction[:, inner_head] - direction[:, inner_tail]  66.7 us
    gather x3, local copies, waits for them, and re-layouts, per_device(): direction[:, inner_tail]  66.6 us
  transfers between devices with their start and end apart: 8, of which 1 were waited for; matrix products, arithmetic and copies ran while one was open for 64% of the time, Pallas kernels for 0%

commit v1 on v0

v1 whole, which is shorter than its diff:
```python
import functools

import jax
import jax.numpy as jnp
from jax import lax
from jax.experimental import pallas as pl
from jax.experimental.pallas import tpu as pltpu
from jax.sharding import PartitionSpec as P

MESH = pl.DeviceIdType.MESH
F32 = jnp.float32
BF16 = jnp.bfloat16
I32 = jnp.int32

TILE = 128
BLOCKS = 32
NODES = 4096
SCEN_ALL = 32
JUNC = 1024
INNER = 6144
SEGS = 7168
SHOWN = 8
CHUNKS = 80
PANEL = 16
GROUP = 16

leak_rate = 0.05
inflow_weight = 20.0


def dot_nt(a, b):
    return lax.dot_general(a, b, (((1,), (1,)), ((), ())), preferred_element_type=F32)


def dot_nn(a, b):
    return lax.dot_general(a, b, (((1,), (0,)), ((), ())), preferred_element_type=F32)


def dot_tn(a, b):
    return lax.dot_general(a, b, (((0,), (0,)), ((), ())), preferred_element_type=F32)


def parts2(x):
    hi = x.astype(BF16).astype(F32)
    return hi, x - hi


def parts3(x):
    hi = x.astype(BF16).astype(F32)
    rest = x - hi
    mid = rest.astype(BF16).astype(F32)
    return hi, mid, rest - mid


def one_hot_rows(row, count):
    ids = lax.broadcasted_iota(I32, (count, row.shape[1]), 0)
    return ids == row


def spread(mask, value):
    return jnp.where(mask, value, 0.0).astype(BF16)


def conductance(radius, seg_length):
    diameter = 2.0 * radius
    power = jnp.exp(0.645 * jnp.log(diameter))
    viscous = 220.0 * jnp.exp(-1.3 * diameter) + 3.2 - 2.44 * jnp.exp(-0.06 * power)
    scaled = diameter * 0.125
    scaled = scaled * scaled
    return scaled * scaled * (50.0 / seg_length) / viscous


def head_kernel(parts, ends, radius, length, live, cond_out, arrived, sent, landed, send_sem, recv_sem):
    place = lax.axis_index("dom")
    upper = lax.rem(place + 1, parts)
    lower = lax.rem(place + parts - 1, parts)
    barrier = pltpu.get_barrier_semaphore()
    for other in (upper, lower):
        pl.semaphore_signal(barrier, inc=1, device_id={"dom": other}, device_id_type=MESH)
    cond = conductance(radius[...], length[...])
    position = lax.broadcasted_iota(I32, (1, SEGS), 1)
    limit = jnp.where(position < INNER, jnp.full((1, SEGS), live[0], I32), jnp.full((1, SEGS), (parts - 1 - place) * SEGS, I32))
    cond = jnp.where(position < limit, cond, 0.0)
    cond_out[...] = cond
    slot = ends[1:2, INNER:]
    junc = cond[:, INNER:]
    owner = one_hot_rows(slot >> 7, SHOWN)
    stack = jnp.concatenate([jnp.where(owner, part, 0.0) for part in parts3(junc)], axis=0).astype(BF16)
    lanes = spread(one_hot_rows(slot & 127, TILE), 1.0)
    sums = dot_nt(stack, lanes)
    sent[...] = sums[0:8] + sums[8:16] + sums[16:24]
    pl.semaphore_wait(barrier, 2)
    copy = pltpu.make_async_remote_copy(
        src_ref=sent, dst_ref=landed, send_sem=send_sem, recv_sem=recv_sem, device_id={"dom": upper}, device_id_type=MESH
    )
    copy.start()
    copy.wait()
    arrived[...] = landed[...]


def setup_kernel(
    ends, cond, mask, shown, arrived, inverse, degree_out, table, rank, degree, sums, packed, counts, counts_smem, sem
):
    degree[...] = jnp.zeros_like(degree)
    sums[...] = jnp.zeros_like(sums)
    width = 256
    before = lax.broadcasted_iota(I32, (width, width), 0) < lax.broadcasted_iota(I32, (width, width), 1)
    before = jnp.where(before, 1.0, 0.0).astype(BF16)

    def add_degree(node, value):
        owner = one_hot_rows(node >> 7, BLOCKS)
        stack = jnp.concatenate([jnp.where(owner, part, 0.0) for part in parts3(value)], axis=0).astype(BF16)
        lanes = spread(one_hot_rows(node & 127, TILE), 1.0)
        degree[...] += dot_nt(stack, lanes)

    def scan(step, carry):
        cols = pl.ds(pl.multiple_of(step * width, width), width)
        head = ends[0:1, cols]
        tail = ends[1:2, cols]
        value = cond[:, cols]
        add_degree(head, value)
        add_degree(tail, value)
        bucket = jnp.where((head >> 7) == (tail >> 7), head >> 7, -1)
        member = one_hot_rows(bucket, BLOCKS)
        ahead = dot_nn(spread(member, 1.0), before)
        rank[:, cols] = jnp.sum(jnp.where(member, ahead + carry, 0.0), axis=0, keepdims=True)
        return carry + jnp.sum(jnp.where(member, 1.0, 0.0), axis=1, keepdims=True)

    total = lax.fori_loop(0, INNER // width, scan, jnp.zeros((BLOCKS, 1), F32))
    add_degree(ends[0:1, INNER:], cond[:, INNER:])
    deg = degree[0:32, :] + degree[32:64, :] + degree[64:96, :]
    block_id = lax.broadcasted_iota(I32, (BLOCKS, TILE), 0)
    for j in range(SHOWN):
        deg = deg + jnp.where(block_id == shown[j], arrived[j : j + 1, :], 0.0)
    deg = deg + (leak_rate + inflow_weight * mask[...].astype(F32))
    degree_out[...] = deg

    chunks = jnp.floor((jnp.broadcast_to(total, (BLOCKS, TILE)) + 127.0) * (1.0 / 128.0))
    below = lax.broadcasted_iota(I32, (BLOCKS, BLOCKS), 1) < lax.broadcasted_iota(I32, (BLOCKS, BLOCKS), 0)
    start = dot_nn(jnp.where(below, 1.0, 0.0).astype(BF16), chunks.astype(BF16))
    counts[0:32, :] = start.astype(I32)
    counts[32:64, :] = chunks.astype(I32)
    to_scalar = pltpu.make_async_copy(counts, counts_smem, sem)
    to_scalar.start()
    start_column = start[:, 0:1]
    wide = 512

    def compact(step, carry):
        cols = pl.ds(pl.multiple_of(step * wide, wide), wide)
        head = ends[0:1, cols]
        tail = ends[1:2, cols]
        inside = (head >> 7) == (tail >> 7)
        bucket = jnp.where(inside, head >> 7, -1)
        base = jnp.sum(jnp.where(one_hot_rows(bucket, BLOCKS), start_column, 0.0), axis=0, keepdims=True)
        order = rank[:, cols].astype(I32)
        chunk = jnp.where(inside, base.astype(I32) + (order >> 7), -1)
        at_chunk = one_hot_rows(chunk, CHUNKS)
        values = ((head & 127).astype(F32), (tail & 127).astype(F32)) + parts3(cond[:, cols])
        stack = jnp.concatenate([spread(at_chunk, value) for value in values], axis=0)
        lanes = spread(one_hot_rows(order & 127, TILE), 1.0)
        sums[...] += dot_nt(stack, lanes)
        return carry

    lax.fori_loop(0, INNER // wide, compact, 0)
    packed[...] = sums[...]
    to_scalar.wait()

    row_id = lax.broadcasted_iota(I32, (TILE, TILE), 0)
    lane_id = lax.broadcasted_iota(I32, (TILE, TILE), 1)

    def fill(block, carry):
        first = counts_smem[block, 0]
        count = counts_smem[block + BLOCKS, 0]

        def add_chunk(index, acc):
            row = first + index
            head = packed[pl.ds(row, 1), :].astype(I32)
            tail = packed[pl.ds(row + CHUNKS, 1), :].astype(I32)
            at_head = row_id == head
            at_tail = row_id == tail
            left = jnp.concatenate([spread(at_head, 1.0), spread(at_tail, 1.0)], axis=1)
            for k in range(3):
                value = packed[pl.ds(row + (2 + k) * CHUNKS, 1), :]
                right = jnp.concatenate([spread(at_tail, value), spread(at_head, value)], axis=1)
                acc = acc + dot_nt(left, right)
            return acc

        acc = lax.fori_loop(0, count, add_chunk, jnp.zeros((TILE, TILE), F32))
        table[block] = jnp.where(row_id == lane_id, degree_out[pl.ds(block, 1), :], -acc)
        return carry

    lax.fori_loop(0, BLOCKS, fill, 0)

    lane16 = lax.broadcasted_iota(I32, (PANEL, TILE), 1)
    row16 = lax.broadcasted_iota(I32, (PANEL, TILE), 0)

    def panel(index, carry):
        base = pl.multiple_of(index * PANEL, PANEL)
        rows = pl.ds(base, PANEL)
        in_panel = (lane_id >= base) & (lane_id < base + PANEL)

        def group(number, inner):
            blocks = [number * GROUP + i for i in range(GROUP)]
            turned = [pltpu.roll(table[b, rows, :], TILE - base, 1) for b in blocks]
            for t in range(PANEL):
                for i in range(GROUP):
                    x = turned[i]
                    pivot = 1.0 / x[t : t + 1, t : t + 1]
                    row = jnp.where(lane16[0:1] == t, pivot, x[t : t + 1, :] * pivot)
                    rest = jnp.where(lane16 == t, 0.0, x) - x[:, t : t + 1] * row
                    turned[i] = jnp.where(row16 == t, row, rest)
            for i, b in enumerate(blocks):
                old = table[b, rows, :]
                new = pltpu.roll(turned[i], base, 1)
                old = jnp.where(lane16 < base, -old, old)
                oh, om, ol = [part.astype(BF16) for part in parts3(old)]
                nh, nm, nl = [part.astype(BF16) for part in parts3(new)]
                left = jnp.concatenate([oh, oh, om, oh, ol, om], axis=0)
                right = jnp.concatenate([nh, nm, nh, nl, nh, nm], axis=0)
                update = dot_tn(left, right)
                table[b] = jnp.where(in_panel, 0.0, table[b]) - update
                table[b, rows, :] = new
            return inner

        lax.fori_loop(0, BLOCKS // GROUP, group, 0)
        return carry

    lax.fori_loop(0, TILE // PANEL, panel, 0)

    def finish(block, carry):
        inverse[block] = table[block].astype(BF16)
        return carry

    lax.fori_loop(0, BLOCKS, finish, 0)


def solve_kernel(
    sizes, inflow, mask, ends, cond, degree, inverse, shown, pressure, mean,
    table, owner8, cond8, basis, images, residual, pair, upper_pair, out, back_out, gathered, fwd_out, fwd_in, back_src, back_in,
    one_buf, two_buf, rep_buf,
    fwd_send, fwd_recv, back_send, back_recv, one_send, one_recv, two_send, two_recv, rep_send, rep_recv,
):
    parts, depth_z, planes, reps = sizes
    place = lax.axis_index("dom")
    mine = lax.axis_index("rep")
    upper = lax.rem(place + 1, parts)
    lower = lax.rem(place + parts - 1, parts)
    core = lax.rem(place, 2)
    column = lax.rem(place // 2, depth_z)
    line = place // (2 * depth_z)
    seat = line * 2 + core

    def plane_place(other):
        return ((other // 2) * depth_z + column) * 2 + lax.rem(other, 2)

    def column_place(other):
        return (line * depth_z + other) * 2 + core

    barrier = pltpu.get_barrier_semaphore()
    partners = [{"dom": upper}, {"dom": lower}]
    partners += [{"dom": plane_place(lax.rem(seat + o, planes))} for o in range(1, planes)]
    partners += [{"dom": column_place(lax.rem(column + o, depth_z))} for o in range(1, depth_z)]
    partners += [{"rep": lax.rem(mine + o, reps)} for o in range(1, reps)]
    for partner in partners:
        pl.semaphore_signal(barrier, inc=1, device_id=partner, device_id_type=MESH)

    wide = 256

    def make(step, carry):
        cols = pl.ds(pl.multiple_of(step * wide, wide), wide)
        value = jnp.broadcast_to(cond[:, cols], (8, wide))
        cond8[:, cols] = value
        for side in range(2):
            node = ends[side : side + 1, cols]
            into = pl.ds(pl.multiple_of(side * SEGS + step * wide, wide), wide)
            table[:, into] = spread(one_hot_rows(node & 127, TILE), 1.0)
            owner8[:, into] = jnp.broadcast_to(node >> 7, (8, wide))
        return carry

    lax.fori_loop(0, SEGS // wide, make, 0)

    def split_into(target, value):
        hi, lo = parts2(value)
        target[:, 0:TILE] = hi.astype(BF16)
        target[:, TILE:] = lo.astype(BF16)

    def gather(source, cols, blocks):
        lanes = table[:, cols]
        full = dot_nn(source[...], jnp.concatenate([lanes, lanes], axis=0))
        owner = owner8[:, cols]
        result = jnp.zeros((8, wide), F32)
        for b in range(blocks):
            result = jnp.where(owner == b, full[8 * b : 8 * b + 8, :], result)
        return result

    def scatter(value, cols, blocks):
        owner = owner8[:, cols]
        hi, lo = parts2(value)
        left = [jnp.concatenate([jnp.where(owner == b, part, 0.0) for b in range(blocks)], axis=0).astype(BF16) for part in (hi, lo)]
        lanes = table[:, cols]
        return dot_nt(jnp.concatenate(left, axis=1), jnp.concatenate([lanes, lanes], axis=1))

    def head_cols(step):
        return pl.ds(pl.multiple_of(step * wide, wide), wide)

    def tail_cols(step):
        return pl.ds(pl.multiple_of(SEGS + step * wide, wide), wide)

    def precondition(k):
        for b in range(BLOCKS):
            field = residual[8 * b : 8 * b + 8, :].astype(BF16)
            basis[k, 8 * b : 8 * b + 8, :] = dot_nn(field, inverse[b])

    for b in range(BLOCKS):
        weight = inflow_weight * mask[b : b + 1, :].astype(F32)
        residual[8 * b : 8 * b + 8, :] = weight * inflow[:, TILE * b : TILE * b + TILE]
    precondition(0)

    lane = lax.broadcasted_iota(I32, (8, TILE), 1)
    moments = jnp.zeros((8, TILE), F32)

    def total_of(k, other):
        acc = jnp.zeros((8, TILE), F32)
        for b in range(BLOCKS):
            acc = acc + basis[k, 8 * b : 8 * b + 8, :] * other(b)
        return jnp.sum(acc, axis=1, keepdims=True)

    def right_side(b):
        weight = inflow_weight * mask[b : b + 1, :].astype(F32)
        return weight * inflow[:, TILE * b : TILE * b + TILE]

    junc_first = INNER // wide
    junc_steps = JUNC // wide
    for k in range(3):
        split_into(pair, basis[k])
        for j in range(SHOWN):
            wanted = jnp.broadcast_to(shown[j : j + 1, :], (8, TILE))
            tile = jnp.zeros((8, TILE), F32)
            for b in range(BLOCKS):
                tile = jnp.where(wanted == b, basis[k, 8 * b : 8 * b + 8, :], tile)
            fwd_out[k, 8 * j : 8 * j + 8, :] = tile
        if k == 0:
            pl.semaphore_wait(barrier, len(partners))
        forward = pltpu.make_async_remote_copy(
            src_ref=fwd_out.at[k], dst_ref=fwd_in.at[k], send_sem=fwd_send.at[k], recv_sem=fwd_recv.at[k],
            device_id={"dom": lower}, device_id_type=MESH,
        )
        forward.start()
        moments = jnp.where(lane == k, total_of(k, right_side), moments)
        if k < 2:
            back_out[...] = jnp.zeros_like(back_out)
            for step in range(junc_steps):
                cols = head_cols(junc_first + step)
                value = gather(pair, cols, BLOCKS)
                gathered[:, step * wide : step * wide + wide] = value
                back_out[...] += scatter(cond8[:, cols] * value, tail_cols(junc_first + step), SHOWN)
            back_src[k] = back_out[...]
            backward = pltpu.make_async_remote_copy(
                src_ref=back_src.at[k], dst_ref=back_in.at[k], send_sem=back_send.at[k], recv_sem=back_recv.at[k],
                device_id={"dom": upper}, device_id_type=MESH,
            )
            backward.start()
            out[...] = jnp.zeros_like(out)

            def inner(step, carry):
                hcols, tcols = head_cols(step), tail_cols(step)
                value = cond8[:, hcols]
                at_head = gather(pair, hcols, BLOCKS)
                at_tail = gather(pair, tcols, BLOCKS)
                out[...] += scatter(value * at_tail, hcols, BLOCKS) + scatter(value * at_head, tcols, BLOCKS)
                return carry

            lax.fori_loop(0, INNER // wide, inner, 0)
            forward.wait()
            split_into(upper_pair, fwd_in[k])
            for step in range(junc_steps):
                hcols, tcols = head_cols(junc_first + step), tail_cols(junc_first + step)
                value = gather(upper_pair, tcols, SHOWN)
                out[...] += scatter(cond8[:, hcols] * value, hcols, BLOCKS)
            backward.wait()
            for b in range(BLOCKS):
                acc = out[8 * b : 8 * b + 8, :]
                for j in range(SHOWN):
                    acc = acc + jnp.where(jnp.broadcast_to(shown[j : j + 1, :], (8, TILE)) == b, back_in[k, 8 * j : 8 * j + 8, :], 0.0)
                image = degree[b : b + 1, :] * basis[k, 8 * b : 8 * b + 8, :] - acc
                images[k, 8 * b : 8 * b + 8, :] = image
                residual[8 * b : 8 * b + 8, :] = residual[8 * b : 8 * b + 8, :] - image
            precondition(k + 1)
            moments = jnp.where(lane == 3 + k, total_of(k, lambda b: images[k, 8 * b : 8 * b + 8, :]), moments)
            moments = jnp.where(lane == 6 + k, total_of(k + 1, lambda b: images[k, 8 * b : 8 * b + 8, :]), moments)
        else:
            def quadratic(step, carry):
                hcols, tcols = head_cols(step), tail_cols(step)
                return carry + cond8[:, hcols] * gather(pair, hcols, BLOCKS) * gather(pair, tcols, BLOCKS)

            crossed = lax.fori_loop(0, INNER // wide, quadratic, jnp.zeros((8, wide), F32))
            forward.wait()
            split_into(upper_pair, fwd_in[k])
            for step in range(junc_steps):
                hcols, tcols = head_cols(junc_first + step), tail_cols(junc_first + step)
                crossed = crossed + cond8[:, hcols] * gather(pair, hcols, BLOCKS) * gather(upper_pair, tcols, SHOWN)
            square = total_of(2, lambda b: degree[b : b + 1, :] * basis[2, 8 * b : 8 * b + 8, :])
            square = square - 2.0 * jnp.sum(crossed, axis=1, keepdims=True)
            moments = jnp.where(lane == 5, square, moments)
            moments = jnp.where(lane == 8, total_of(2, lambda b: images[0, 8 * b : 8 * b + 8, :]), moments)

    def exchange(buffer, send, recv, index, count, target):
        copies = []
        for o in range(1, count):
            other = lax.rem(index + o, count)
            copies.append(pltpu.make_async_remote_copy(
                src_ref=buffer.at[index], dst_ref=buffer.at[index], send_sem=send.at[o], recv_sem=recv.at[o],
                device_id=target(other), device_id_type=MESH,
            ))
        for copy in copies:
            copy.start()
        for copy in copies:
            copy.wait()
        acc = buffer[0]
        for o in range(1, count):
            acc = acc + buffer[o]
        return acc

    one_buf[seat] = moments
    moments = exchange(one_buf, one_send, one_recv, seat, planes, lambda other: {"dom": plane_place(other)})
    two_buf[column] = moments
    moments = exchange(two_buf, two_send, two_recv, column, depth_z, lambda other: {"dom": column_place(other)})

    def entry(index):
        return jnp.broadcast_to(moments[:, index : index + 1], (8, TILE))

    b0, b1, b2, g00, g11, g22, g01, g12, g02 = [entry(i) for i in range(9)]

    def safe_inverse(value, scale):
        good = value > 1e-6 * scale
        return jnp.where(good, 1.0 / jnp.where(good, value, 1.0), 0.0)

    i0 = safe_inverse(g00, g00)
    l10 = g01 * i0
    l20 = g02 * i0
    i1 = safe_inverse(g11 - l10 * g01, g11)
    c12 = g12 - l20 * g01
    l21 = c12 * i1
    i2 = safe_inverse(g22 - l20 * g02 - l21 * c12, g22)
    w1 = b1 - l10 * b0
    w2 = b2 - l20 * b0 - l21 * w1
    y2 = w2 * i2
    y1 = w1 * i1 - l21 * y2
    y0 = b0 * i0 - l10 * y1 - l20 * y2
    for b in range(BLOCKS):
        rows = slice(8 * b, 8 * b + 8)
        value = y0 * basis[0, rows, :] + y1 * basis[1, rows, :] + y2 * basis[2, rows, :]
        pressure[:, TILE * b : TILE * b + TILE] = value
        rep_buf[mine, b : b + 1, :] = jnp.sum(value, axis=0, keepdims=True)
    total = exchange(rep_buf, rep_send, rep_recv, mine, reps, lambda other: {"rep": other})
    mean[...] = total * (1.0 / SCEN_ALL)


def vmem(count):
    return [pl.BlockSpec(memory_space=pltpu.VMEM)] * count


def smem(count):
    return [pl.BlockSpec(memory_space=pltpu.SMEM)] * count


def per_device(sizes, inflow, mask, ends, live, shown, radius, length):
    parts, depth_z, planes, reps = sizes
    mask = mask.reshape(BLOCKS, TILE)
    dma = pltpu.SemaphoreType.DMA
    cond, arrived = pl.pallas_call(
        functools.partial(head_kernel, parts),
        out_shape=(jax.ShapeDtypeStruct((1, SEGS), F32), jax.ShapeDtypeStruct((SHOWN, TILE), F32)),
        in_specs=vmem(3) + smem(1),
        out_specs=tuple(vmem(2)),
        scratch_shapes=[pltpu.VMEM((SHOWN, TILE), F32), pltpu.VMEM((SHOWN, TILE), F32), dma, dma],
        compiler_params=pltpu.CompilerParams(collective_id=0, has_side_effects=True),
        name="conductances",
    )(ends, radius.reshape(1, SEGS), length.reshape(1, SEGS), live)
    inverse, degree = pl.pallas_call(
        setup_kernel,
        out_shape=(jax.ShapeDtypeStruct((BLOCKS, TILE, TILE), BF16), jax.ShapeDtypeStruct((BLOCKS, TILE), F32)),
        in_specs=vmem(3) + smem(1) + vmem(1),
        out_specs=tuple(vmem(2)),
        scratch_shapes=[
            pltpu.VMEM((BLOCKS, TILE, TILE), F32),
            pltpu.VMEM((1, INNER), F32),
            pltpu.VMEM((96, TILE), F32),
            pltpu.VMEM((5 * CHUNKS, TILE), F32),
            pltpu.VMEM((5 * CHUNKS, TILE), F32),
            pltpu.VMEM((64, TILE), I32),
            pltpu.SMEM((64, TILE), I32),
            dma,
        ],
        name="inverses",
    )(ends, cond, mask, shown, arrived)
    rows = 8 * BLOCKS
    back = 8 * SHOWN
    pressure, mean = pl.pallas_call(
        functools.partial(solve_kernel, sizes),
        out_shape=(jax.ShapeDtypeStruct((8, NODES), F32), jax.ShapeDtypeStruct((BLOCKS, TILE), F32)),
        in_specs=vmem(7),
        out_specs=tuple(vmem(2)),
        scratch_shapes=[
            pltpu.VMEM((TILE, 2 * SEGS), BF16),
            pltpu.VMEM((8, 2 * SEGS), I32),
            pltpu.VMEM((8, SEGS), F32),
            pltpu.VMEM((3, rows, TILE), F32),
            pltpu.VMEM((2, rows, TILE), F32),
            pltpu.VMEM((rows, TILE), F32),
            pltpu.VMEM((rows, 2 * TILE), BF16),
            pltpu.VMEM((back, 2 * TILE), BF16),
            pltpu.VMEM((rows, TILE), F32),
            pltpu.VMEM((back, TILE), F32),
            pltpu.VMEM((8, JUNC), F32),
            pltpu.VMEM((3, back, TILE), F32),
            pltpu.VMEM((3, back, TILE), F32),
            pltpu.VMEM((2, back, TILE), F32),
            pltpu.VMEM((2, back, TILE), F32),
            pltpu.VMEM((planes, 8, TILE), F32),
            pltpu.VMEM((depth_z, 8, TILE), F32),
            pltpu.VMEM((reps, BLOCKS, TILE), F32),
            dma((3,)), dma((3,)), dma((2,)), dma((2,)),
            dma((planes,)), dma((planes,)), dma((depth_z,)), dma((depth_z,)), dma((reps,)), dma((reps,)),
        ],
        compiler_params=pltpu.CompilerParams(collective_id=1, has_side_effects=True),
        name="gradients",
    )(inflow, mask, ends, cond, degree, inverse, jnp.broadcast_to(shown[:, None], (SHOWN, TILE)))
    return pressure, mean.reshape(NODES)


def solution(mesh):
    in_specs = (P("rep", "dom"), P("dom"), P(None, "dom"), P("dom"), P("dom"), P("dom"), P("dom"))
    out_specs = (P("rep", "dom"), P("dom"))
    parts, reps = mesh.shape["dom"], mesh.shape["rep"]
    depth_z = 8 if parts == 64 else parts // 4
    sizes = (parts, depth_z, parts // depth_z, reps)
    return jax.shard_map(
        functools.partial(per_device, sizes), mesh=mesh, in_specs=in_specs, out_specs=out_specs, check_vma=False
    )
```

time: 2020 us -> 186 us (0.09)
  other arithmetic: 1150 us -> 0 us
  blocking collectives: 638 us -> 0 us
  local copies, waits for them, and re-layouts: 189 us -> 3.49 us
  Pallas kernels: 0 us -> 180 us
  starting transfers between devices: 23.4 us -> 0 us
    another operation x7 -> x0, other arithmetic: 693 us -> none  [the longest x4 376 us: one_group(): factor = jnp.linalg.cholesky(tiles)]
    psum x6 -> x0, blocking collectives: 638 us -> none  [the longest x3 378 us: residual_product(): return lax.psum(jnp.sum(residual * z_field, axis=1), 'dom')]
    scatter-add x22 -> x0, other arithmetic: 434 us -> none  [the longest x9 260 us: per_device(): out = out.at[:, inner_head].add(inner_flow).at[:, inner_tail].add(-inner_...]
    pallas_call x0 -> x3, Pallas kernels: none -> 180 us  [the longest x1 117 us: per_device(): pl.pallas_call(setup_kernel, out_shape=(jax.ShapeDtypeStruct((BLOCKS, TIL...]
    gather x15 -> x0, local copies, waits for them, and re-layouts: 163 us -> none  [the longest x3 66.7 us: per_device(): direction[:, inner_head] - direction[:, inner_tail]]
    ppermute x8 -> x0, starting transfers between devices: 23.4 us -> none  [passed_along(): lax.ppermute(value, axis, [(source, source + steps) for source in range(i...]
  transfers between devices with their start and end apart: 8 -> 0, of which waited for: 1 -> 0; matrix products, arithmetic and copies ran while one was open for 64% -> 0% of each run, Pallas kernels for 0% -> 0%
where the time goes in v1:
time: 186 us; the launch traced here: 185 us
  Pallas kernels  180 us (97%)
  local copies, waits for them, and re-layouts  3.49 us (2%)
    pallas_call x1, Pallas kernels, per_device(): pl.pallas_call(setup_kernel, out_shape=(jax.ShapeDtypeStruct((BLOCKS, TIL...  117 us
    pallas_call x1, Pallas kernels, per_device(): pl.pallas_call(functools.partial(solve_kernel, sizes), out_shape=(jax.Sha...  51.6 us
    pallas_call x1, Pallas kernels, per_device(): pl.pallas_call(functools.partial(head_kernel, parts), out_shape=(jax.Shap...  11.4 us

profile of v1, /device:TPU:1, one launch (start us, length us, event | category | flops | bytes accessed | tf_op | source)
XLA Modules:
  0.0 185.1 jit_solution(2414029800780762127)
XLA Ops:
  1.3 0.0 copy-start.1
  1.3 0.6 copy-done.1
  1.9 0.7 broadcast_in_dim.2.shown
  2.6 11.4 %conductances.1 = (f32[1,7168]{1,0:T(1,128)}, f32[8,128]{1,0:T(8,128)}) custom-call(s32[2,7168]{1,0:T(2,128)} %ends.5, f32[1,7168]{1,0:T(1,128)} %bitcast.6, f32[1,7168]{1,0:T(1,128)} %bitcast.7, s32[1]{0:T(128)S(6)} %copy.11.live), custom_call_target="tpu_custom_call" | custom-call | tf_op jit(solution)/shard_map/conductances/pallas_call | solution.py:471
  14.0 117.3 %inverses.1 = (bf16[32,128,128]{2,1,0:T(8,128)(2,1)}, f32[32,128]{1,0:T(8,128)}) custom-call(s32[2,7168]{1,0:T(2,128)} %ends.5, f32[1,7168]{1,0:T(1,128)} %get-tuple-element.8.cond, s32[32,128]{1,0:T(8,128)} %bitcast.4, s32[8]{0:T(128)} %shown.1, f32[8,128]{1,0:T(8,128)} %get-tuple-element.9.arrived), custom_call_target="tpu_custom_call" | custom-call | tf_op jit(solution)/shard_map/inverses/pallas_call | solution.py:480
  131.3 51.6 %gradients.1 = (f32[8,4096]{1,0:T(8,128)}, f32[32,128]{1,0:T(8,128)}) custom-call(f32[8,4096]{1,0:T(8,128)} %inflow.1, s32[32,128]{1,0:T(8,128)} %bitcast.5, s32[2,7168]{1,0:T(2,128)} %ends.5, f32[1,7168]{1,0:T(1,128)} %get-tuple-element.8.cond, f32[32,128]{1,0:T(8,128)} %get-tuple-element.10.degree, bf16[32,128,128]{2,1,0:T(8,128)(2,1)} %get-tuple-element.11.inverse, ...), custom_call_target="tpu_custom_call" | custom-call | tf_op jit(solution)/shard_map/gradients/pallas_call | solution.py:499
  182.9 0.0 copy-start
  182.9 1.6 copy.12
  184.5 0.0 copy-done
  184.5 0.6 copy.13
Async XLA Ops:
  1.3 0.7 copy-start.1
  182.9 1.6 copy-start

commit v2 on v1

--- a/solution.py
+++ b/solution.py
@@ -21,8 +21,9 @@
 SEGS = 7168
 SHOWN = 8
 CHUNKS = 80
-PANEL = 16
-GROUP = 16
+PANEL = 32
+FOUR = 4
+UNROLL = 4
 
 leak_rate = 0.05
 inflow_weight = 20.0
@@ -191,38 +192,64 @@
 
     lax.fori_loop(0, BLOCKS, fill, 0)
 
-    lane16 = lax.broadcasted_iota(I32, (PANEL, TILE), 1)
-    row16 = lax.broadcasted_iota(I32, (PANEL, TILE), 0)
+    panel_lane = lax.broadcasted_iota(I32, (PANEL, TILE), 1)
+    panel_row = lax.broadcasted_iota(I32, (PANEL, TILE), 0)
+    own_lane = panel_lane & (PANEL - 1)
+    own_block = (row_id // PANEL) == (lane_id // PANEL)
 
     def panel(index, carry):
         base = pl.multiple_of(index * PANEL, PANEL)
         rows = pl.ds(base, PANEL)
-        in_panel = (lane_id >= base) & (lane_id < base + PANEL)
-
-        def group(number, inner):
-            blocks = [number * GROUP + i for i in range(GROUP)]
-            turned = [pltpu.roll(table[b, rows, :], TILE - base, 1) for b in blocks]
-            for t in range(PANEL):
-                for i in range(GROUP):
-                    x = turned[i]
-                    pivot = 1.0 / x[t : t + 1, t : t + 1]
-                    row = jnp.where(lane16[0:1] == t, pivot, x[t : t + 1, :] * pivot)
-                    rest = jnp.where(lane16 == t, 0.0, x) - x[:, t : t + 1] * row
-                    turned[i] = jnp.where(row16 == t, row, rest)
-            for i, b in enumerate(blocks):
-                old = table[b, rows, :]
-                new = pltpu.roll(turned[i], base, 1)
-                old = jnp.where(lane16 < base, -old, old)
-                oh, om, ol = [part.astype(BF16) for part in parts3(old)]
-                nh, nm, nl = [part.astype(BF16) for part in parts3(new)]
-                left = jnp.concatenate([oh, oh, om, oh, ol, om], axis=0)
-                right = jnp.concatenate([nh, nm, nh, nl, nh, nm], axis=0)
-                update = dot_tn(left, right)
-                table[b] = jnp.where(in_panel, 0.0, table[b]) - update
-                table[b, rows, :] = new
-            return inner
-
-        lax.fori_loop(0, BLOCKS // GROUP, group, 0)
+        olds = [table[b, rows, :] for b in range(BLOCKS)]
+        small = []
+        for g in range(BLOCKS // FOUR):
+            joined = jnp.zeros((PANEL, TILE), F32)
+            for i in range(FOUR):
+                turned = pltpu.roll(olds[g * FOUR + i], lax.rem(PANEL * i + TILE - base, TILE), 1)
+                joined = jnp.where((panel_lane // PANEL) == i, turned, joined)
+            small.append(joined)
+        for t in range(PANEL):
+            source = (panel_lane // PANEL) * PANEL + t
+            at_lane = own_lane == t
+            for g in range(BLOCKS // FOUR):
+                x = small[g]
+                column = jnp.take_along_axis(x, source, axis=1, mode="promise_in_bounds")
+                pivot = 1.0 / column[t : t + 1, :]
+                row = jnp.where(at_lane[0:1], pivot, x[t : t + 1, :] * pivot)
+                rest = jnp.where(at_lane, 0.0, x) - column * row
+                small[g] = jnp.where(panel_row == t, row, rest)
+        unit = jnp.where(panel_lane == panel_row + base, 1.0, 0.0)
+        in_panel = (panel_lane >= base) & (panel_lane < base + PANEL)
+        keep = ((lane_id >= base) & (lane_id < base + PANEL)) | ((row_id >= base) & (row_id < base + PANEL))
+        zero = jnp.zeros((PANEL, TILE), BF16)
+        for g in range(BLOCKS // FOUR):
+            diagonal = jnp.where(own_block, jnp.concatenate([small[g]] * FOUR, axis=0), 0.0)
+            members = [jnp.where(in_panel, unit, olds[g * FOUR + i]) for i in range(FOUR)]
+            stack = jnp.concatenate(members, axis=0)
+            dh, dm, dl = [part.astype(BF16) for part in parts3(diagonal)]
+            sh, sm, sl = [part.astype(BF16) for part in parts3(stack)]
+            fresh = dot_nn(jnp.concatenate([dh, dm], axis=1), jnp.concatenate([sh, sm], axis=0))
+            fresh = fresh + dot_nn(jnp.concatenate([dh, dm], axis=1), jnp.concatenate([sm, sh], axis=0))
+            fresh = fresh + dot_nn(jnp.concatenate([dh, dl], axis=1), jnp.concatenate([sl, sh], axis=0))
+            turned = jnp.where(row_id < base + PANEL, -stack.T, stack.T)
+            th, tm, tl = [part.astype(BF16) for part in parts3(turned)]
+            fh, fm, fl = [part.astype(BF16) for part in parts3(fresh)]
+
+            def across(value):
+                lines = []
+                for i in range(FOUR):
+                    cells = [zero] * FOUR
+                    cells[i] = value[PANEL * i : PANEL * i + PANEL, :]
+                    lines.append(jnp.concatenate(cells, axis=1))
+                return jnp.concatenate(lines, axis=0)
+
+            ah, am, al = across(fh), across(fm), across(fl)
+            update = dot_nn(jnp.concatenate([th, tm], axis=1), jnp.concatenate([ah, am], axis=0))
+            update = update + dot_nn(jnp.concatenate([th, tm], axis=1), jnp.concatenate([am, ah], axis=0))
+            update = update + dot_nn(jnp.concatenate([th, tl], axis=1), jnp.concatenate([al, ah], axis=0))
+            for i in range(FOUR):
+                b = g * FOUR + i
+                table[b] = jnp.where(keep, 0.0, table[b]) - update[:, TILE * i : TILE * i + TILE]
         return carry
 
     lax.fori_loop(0, TILE // PANEL, panel, 0)
@@ -236,7 +263,7 @@
 
 def solve_kernel(
     sizes, inflow, mask, ends, cond, degree, inverse, shown, pressure, mean,
-    table, owner8, cond8, basis, images, residual, pair, upper_pair, out, back_out, gathered, fwd_out, fwd_in, back_src, back_in,
+    table, owner8, cond8, basis, images, residual, pair, upper_pair, out, back_out, fwd_out, fwd_in, back_src, back_in,
     one_buf, two_buf, rep_buf,
     fwd_send, fwd_recv, back_send, back_recv, one_send, one_recv, two_send, two_recv, rep_send, rep_recv,
 ):
@@ -273,32 +300,46 @@
         for side in range(2):
             node = ends[side : side + 1, cols]
             into = pl.ds(pl.multiple_of(side * SEGS + step * wide, wide), wide)
-            table[:, into] = spread(one_hot_rows(node & 127, TILE), 1.0)
-            owner8[:, into] = jnp.broadcast_to(node >> 7, (8, wide))
+            table[:, into] = spread(one_hot_rows(node & 255, 256), 1.0)
+            owner8[:, into] = jnp.broadcast_to(node >> 8, (8, wide))
         return carry
 
     lax.fori_loop(0, SEGS // wide, make, 0)
 
-    def split_into(target, value):
-        hi, lo = parts2(value)
-        target[:, 0:TILE] = hi.astype(BF16)
-        target[:, TILE:] = lo.astype(BF16)
-
-    def gather(source, cols, blocks):
-        lanes = table[:, cols]
-        full = dot_nn(source[...], jnp.concatenate([lanes, lanes], axis=0))
+    def split_into(target, tile, pairs):
+        rows = 8 * pairs
+        for q in range(0, pairs, 2):
+            highs, lows = [], []
+            for half in range(2):
+                parts = [parts2(tile(2 * (q + i) + half)) for i in range(2)]
+                highs.append(jnp.concatenate([part[0] for part in parts], axis=0))
+                lows.append(jnp.concatenate([part[1] for part in parts], axis=0))
+            target[8 * q : 8 * q + 16, :] = jnp.concatenate(highs, axis=1).astype(BF16)
+            target[rows + 8 * q : rows + 8 * q + 16, :] = jnp.concatenate(lows, axis=1).astype(BF16)
+
+    def gather(source, cols, pairs):
+        full = dot_nn(source[...], table[:, cols])
         owner = owner8[:, cols]
         result = jnp.zeros((8, wide), F32)
-        for b in range(blocks):
-            result = jnp.where(owner == b, full[8 * b : 8 * b + 8, :], result)
+        for q in range(pairs):
+            value = full[8 * q : 8 * q + 8, :] + full[8 * (q + pairs) : 8 * (q + pairs) + 8, :]
+            result = jnp.where(owner == q, value, result)
         return result
 
-    def scatter(value, cols, blocks):
-        owner = owner8[:, cols]
-        hi, lo = parts2(value)
-        left = [jnp.concatenate([jnp.where(owner == b, part, 0.0) for b in range(blocks)], axis=0).astype(BF16) for part in (hi, lo)]
-        lanes = table[:, cols]
-        return dot_nt(jnp.concatenate(left, axis=1), jnp.concatenate([lanes, lanes], axis=1))
+    def scatter(values, cols, pairs):
+        left, right = [], []
+        for value, at in zip(values, cols):
+            owner = owner8[:, at]
+            left.append(jnp.concatenate([jnp.where(owner == q, part, 0.0) for part in parts2(value) for q in range(pairs)], axis=0).astype(BF16))
+            right.append(table[:, at])
+        return dot_nt(jnp.concatenate(left, axis=1), jnp.concatenate(right, axis=1))
+
+    def tile_of(source, b, pairs):
+        rows, lanes = 8 * (b // 2), slice(TILE * (b % 2), TILE * (b % 2) + TILE)
+        return source[rows : rows + 8, lanes] + source[8 * pairs + rows : 8 * pairs + rows + 8, lanes]
+
+    pairs_all = BLOCKS // 2
+    pairs_shown = SHOWN // 2
 
     def head_cols(step):
         return pl.ds(pl.multiple_of(step * wide, wide), wide)
@@ -332,7 +373,7 @@
     junc_first = INNER // wide
     junc_steps = JUNC // wide
     for k in range(3):
-        split_into(pair, basis[k])
+        split_into(pair, lambda b: basis[k, 8 * b : 8 * b + 8, :], pairs_all)
         for j in range(SHOWN):
             wanted = jnp.broadcast_to(shown[j : j + 1, :], (8, TILE))
             tile = jnp.zeros((8, TILE), F32)
@@ -348,13 +389,11 @@
         forward.start()
         moments = jnp.where(lane == k, total_of(k, right_side), moments)
         if k < 2:
-            back_out[...] = jnp.zeros_like(back_out)
-            for step in range(junc_steps):
-                cols = head_cols(junc_first + step)
-                value = gather(pair, cols, BLOCKS)
-                gathered[:, step * wide : step * wide + wide] = value
-                back_out[...] += scatter(cond8[:, cols] * value, tail_cols(junc_first + step), SHOWN)
-            back_src[k] = back_out[...]
+            hcols = [head_cols(junc_first + step) for step in range(junc_steps)]
+            tcols = [tail_cols(junc_first + step) for step in range(junc_steps)]
+            back_out[...] = scatter([cond8[:, at] * gather(pair, at, pairs_all) for at in hcols], tcols, pairs_shown)
+            for j in range(SHOWN):
+                back_src[k, 8 * j : 8 * j + 8, :] = tile_of(back_out, j, pairs_shown)
             backward = pltpu.make_async_remote_copy(
                 src_ref=back_src.at[k], dst_ref=back_in.at[k], send_sem=back_send.at[k], recv_sem=back_recv.at[k],
                 device_id={"dom": upper}, device_id_type=MESH,
@@ -363,23 +402,22 @@
             out[...] = jnp.zeros_like(out)
 
             def inner(step, carry):
-                hcols, tcols = head_cols(step), tail_cols(step)
-                value = cond8[:, hcols]
-                at_head = gather(pair, hcols, BLOCKS)
-                at_tail = gather(pair, tcols, BLOCKS)
-                out[...] += scatter(value * at_tail, hcols, BLOCKS) + scatter(value * at_head, tcols, BLOCKS)
+                values, cols = [], []
+                for i in range(UNROLL):
+                    h, t = head_cols(UNROLL * step + i), tail_cols(UNROLL * step + i)
+                    weight = cond8[:, h]
+                    values += [weight * gather(pair, t, pairs_all), weight * gather(pair, h, pairs_all)]
+                    cols += [h, t]
+                out[...] += scatter(values, cols, pairs_all)
                 return carry
 
-            lax.fori_loop(0, INNER // wide, inner, 0)
+            lax.fori_loop(0, INNER // wide // UNROLL, inner, 0)
             forward.wait()
-            split_into(upper_pair, fwd_in[k])
-            for step in range(junc_steps):
-                hcols, tcols = head_cols(junc_first + step), tail_cols(junc_first + step)
-                value = gather(upper_pair, tcols, SHOWN)
-                out[...] += scatter(cond8[:, hcols] * value, hcols, BLOCKS)
+            split_into(upper_pair, lambda j: fwd_in[k, 8 * j : 8 * j + 8, :], pairs_shown)
+            out[...] += scatter([cond8[:, h] * gather(upper_pair, t, pairs_shown) for h, t in zip(hcols, tcols)], hcols, pairs_all)
             backward.wait()
             for b in range(BLOCKS):
-                acc = out[8 * b : 8 * b + 8, :]
+                acc = tile_of(out, b, pairs_all)
                 for j in range(SHOWN):
                     acc = acc + jnp.where(jnp.broadcast_to(shown[j : j + 1, :], (8, TILE)) == b, back_in[k, 8 * j : 8 * j + 8, :], 0.0)
                 image = degree[b : b + 1, :] * basis[k, 8 * b : 8 * b + 8, :] - acc
@@ -390,15 +428,17 @@
             moments = jnp.where(lane == 6 + k, total_of(k + 1, lambda b: images[k, 8 * b : 8 * b + 8, :]), moments)
         else:
             def quadratic(step, carry):
-                hcols, tcols = head_cols(step), tail_cols(step)
-                return carry + cond8[:, hcols] * gather(pair, hcols, BLOCKS) * gather(pair, tcols, BLOCKS)
-
-            crossed = lax.fori_loop(0, INNER // wide, quadratic, jnp.zeros((8, wide), F32))
+                for i in range(UNROLL):
+                    h, t = head_cols(UNROLL * step + i), tail_cols(UNROLL * step + i)
+                    carry = carry + cond8[:, h] * gather(pair, h, pairs_all) * gather(pair, t, pairs_all)
+                return carry
+
+            crossed = lax.fori_loop(0, INNER // wide // UNROLL, quadratic, jnp.zeros((8, wide), F32))
+            ahead = [cond8[:, head_cols(junc_first + step)] * gather(pair, head_cols(junc_first + step), pairs_all) for step in range(junc_steps)]
             forward.wait()
-            split_into(upper_pair, fwd_in[k])
+            split_into(upper_pair, lambda j: fwd_in[k, 8 * j : 8 * j + 8, :], pairs_shown)
             for step in range(junc_steps):
-                hcols, tcols = head_cols(junc_first + step), tail_cols(junc_first + step)
-                crossed = crossed + cond8[:, hcols] * gather(pair, hcols, BLOCKS) * gather(upper_pair, tcols, SHOWN)
+                crossed = crossed + ahead[step] * gather(upper_pair, tail_cols(junc_first + step), pairs_shown)
             square = total_of(2, lambda b: degree[b : b + 1, :] * basis[2, 8 * b : 8 * b + 8, :])
             square = square - 2.0 * jnp.sum(crossed, axis=1, keepdims=True)
             moments = jnp.where(lane == 5, square, moments)
@@ -502,7 +542,7 @@
         in_specs=vmem(7),
         out_specs=tuple(vmem(2)),
         scratch_shapes=[
-            pltpu.VMEM((TILE, 2 * SEGS), BF16),
+            pltpu.VMEM((2 * TILE, 2 * SEGS), BF16),
             pltpu.VMEM((8, 2 * SEGS), I32),
             pltpu.VMEM((8, SEGS), F32),
             pltpu.VMEM((3, rows, TILE), F32),
@@ -510,9 +550,8 @@
             pltpu.VMEM((rows, TILE), F32),
             pltpu.VMEM((rows, 2 * TILE), BF16),
             pltpu.VMEM((back, 2 * TILE), BF16),
-            pltpu.VMEM((rows, TILE), F32),
-            pltpu.VMEM((back, TILE), F32),
-            pltpu.VMEM((8, JUNC), F32),
+            pltpu.VMEM((rows, 2 * TILE), F32),
+            pltpu.VMEM((back, 2 * TILE), F32),
             pltpu.VMEM((3, back, TILE), F32),
             pltpu.VMEM((3, back, TILE), F32),
             pltpu.VMEM((2, back, TILE), F32),

time: 186 us -> 100 us (0.54)
  Pallas kernels: 180 us -> 95.3 us
    pallas_call x1, Pallas kernels: 117 us -> 49 us  [per_device(): pl.pallas_call(setup_kernel, out_shape=(jax.ShapeDtypeStruct((BLOCKS, TIL...]
    pallas_call x1, Pallas kernels: 51.6 us -> 34.9 us  [per_device(): pl.pallas_call(functools.partial(solve_kernel, sizes), out_shape=(jax.Sha...]
where the time goes in v2:
time: 100 us
  Pallas kernels  95.3 us (95%)
  local copies, waits for them, and re-layouts  3.49 us (3%)
  between operations  1.32 us (1%)
    pallas_call x1, Pallas kernels, per_device(): pl.pallas_call(setup_kernel, out_shape=(jax.ShapeDtypeStruct((BLOCKS, TIL...  49 us
    pallas_call x1, Pallas kernels, per_device(): pl.pallas_call(functools.partial(solve_kernel, sizes), out_shape=(jax.Sha...  34.9 us
    pallas_call x1, Pallas kernels, per_device(): pl.pallas_call(functools.partial(head_kernel, parts), out_shape=(jax.Shap...  11.4 us
    unnamed x6, local copies, waits for them, and re-layouts  2.83 us

profile of v2, /device:TPU:1, one launch (start us, length us, event | category | flops | bytes accessed | tf_op | source)
XLA Modules:
  0.0 100.1 jit_solution(17319144396257115316)
XLA Ops:
  1.3 0.0 copy-start.1
  1.3 0.6 copy-done.1
  1.9 0.7 broadcast_in_dim.2.shown
  2.6 11.4 %conductances.1 = (f32[1,7168]{1,0:T(1,128)}, f32[8,128]{1,0:T(8,128)}) custom-call(s32[2,7168]{1,0:T(2,128)} %ends.5, f32[1,7168]{1,0:T(1,128)} %bitcast.6, f32[1,7168]{1,0:T(1,128)} %bitcast.7, s32[1]{0:T(128)S(6)} %copy.11.live), custom_call_target="tpu_custom_call" | custom-call | tf_op jit(solution)/shard_map/conductances/pallas_call | solution.py:511
  14.0 49.0 %inverses.1 = (bf16[32,128,128]{2,1,0:T(8,128)(2,1)}, f32[32,128]{1,0:T(8,128)}) custom-call(s32[2,7168]{1,0:T(2,128)} %ends.5, f32[1,7168]{1,0:T(1,128)} %get-tuple-element.8.cond, s32[32,128]{1,0:T(8,128)} %bitcast.4, s32[8]{0:T(128)} %shown.1, f32[8,128]{1,0:T(8,128)} %get-tuple-element.9.arrived), custom_call_target="tpu_custom_call" | custom-call | tf_op jit(solution)/shard_map/inverses/pallas_call | solution.py:520
  63.0 34.9 %gradients.1 = (f32[8,4096]{1,0:T(8,128)}, f32[32,128]{1,0:T(8,128)}) custom-call(f32[8,4096]{1,0:T(8,128)} %inflow.1, s32[32,128]{1,0:T(8,128)} %bitcast.5, s32[2,7168]{1,0:T(2,128)} %ends.5, f32[1,7168]{1,0:T(1,128)} %get-tuple-element.8.cond, f32[32,128]{1,0:T(8,128)} %get-tuple-element.10.degree, bf16[32,128,128]{2,1,0:T(8,128)(2,1)} %get-tuple-element.11.inverse, ...), custom_call_target="tpu_custom_call" | custom-call | tf_op jit(solution)/shard_map/gradients/pallas_call | solution.py:539
  97.9 0.0 copy-start
  97.9 1.6 %copy.12 = f32[8,4096]{1,0:T(8,128)} copy(f32[8,4096]{1,0:T(8,128)} %get-tuple-element.16) | data formatting | bytes 262144
  99.5 0.0 copy-done
  99.5 0.6 copy.13
Async XLA Ops:
  1.3 0.7 copy-start.1
  97.9 1.6 %copy-start = (f32[32,128]{1,0:T(8,128)S(1)}, f32[32,128]{1,0:T(8,128)}, u32[]{:S(2)}) copy-start(f32[32,128]{1,0:T(8,128)} %get-tuple-element.13) | copy-start | bytes 49156

commit v3 on v2

--- a/solution.py
+++ b/solution.py
@@ -24,6 +24,7 @@
 PANEL = 32
 FOUR = 4
 UNROLL = 4
+SCANS = 2
 
 leak_rate = 0.05
 inflow_weight = 20.0
@@ -82,14 +83,16 @@
     position = lax.broadcasted_iota(I32, (1, SEGS), 1)
     limit = jnp.where(position < INNER, jnp.full((1, SEGS), live[0], I32), jnp.full((1, SEGS), (parts - 1 - place) * SEGS, I32))
     cond = jnp.where(position < limit, cond, 0.0)
+    high, low = parts2(cond)
+    cond = high + low.astype(BF16).astype(F32)
     cond_out[...] = cond
     slot = ends[1:2, INNER:]
     junc = cond[:, INNER:]
     owner = one_hot_rows(slot >> 7, SHOWN)
-    stack = jnp.concatenate([jnp.where(owner, part, 0.0) for part in parts3(junc)], axis=0).astype(BF16)
+    stack = jnp.concatenate([jnp.where(owner, part, 0.0) for part in parts2(junc)], axis=0).astype(BF16)
     lanes = spread(one_hot_rows(slot & 127, TILE), 1.0)
     sums = dot_nt(stack, lanes)
-    sent[...] = sums[0:8] + sums[8:16] + sums[16:24]
+    sent[...] = sums[0:8] + sums[8:16]
     pl.semaphore_wait(barrier, 2)
     copy = pltpu.make_async_remote_copy(
         src_ref=sent, dst_ref=landed, send_sem=send_sem, recv_sem=recv_sem, device_id={"dom": upper}, device_id_type=MESH
@@ -100,7 +103,7 @@
 
 
 def setup_kernel(
-    ends, cond, mask, shown, arrived, inverse, degree_out, table, rank, degree, sums, packed, counts, counts_smem, sem
+    ends, cond, mask, shown, arrived, inverse, degree_out, table, rank, degree, sums, packed, counts, old_rows, turned_rows, small, counts_smem, sem
 ):
     degree[...] = jnp.zeros_like(degree)
     sums[...] = jnp.zeros_like(sums)
@@ -108,28 +111,34 @@
     before = lax.broadcasted_iota(I32, (width, width), 0) < lax.broadcasted_iota(I32, (width, width), 1)
     before = jnp.where(before, 1.0, 0.0).astype(BF16)
 
-    def add_degree(node, value):
-        owner = one_hot_rows(node >> 7, BLOCKS)
-        stack = jnp.concatenate([jnp.where(owner, part, 0.0) for part in parts3(value)], axis=0).astype(BF16)
-        lanes = spread(one_hot_rows(node & 127, TILE), 1.0)
-        degree[...] += dot_nt(stack, lanes)
+    def add_degree(nodes, values):
+        stacks, lanes = [], []
+        for node, value in zip(nodes, values):
+            owner = one_hot_rows(node >> 7, BLOCKS)
+            stacks.append(jnp.concatenate([jnp.where(owner, part, 0.0) for part in parts2(value)], axis=0).astype(BF16))
+            lanes.append(spread(one_hot_rows(node & 127, TILE), 1.0))
+        degree[...] += dot_nt(jnp.concatenate(stacks, axis=1), jnp.concatenate(lanes, axis=1))
 
     def scan(step, carry):
-        cols = pl.ds(pl.multiple_of(step * width, width), width)
-        head = ends[0:1, cols]
-        tail = ends[1:2, cols]
-        value = cond[:, cols]
-        add_degree(head, value)
-        add_degree(tail, value)
-        bucket = jnp.where((head >> 7) == (tail >> 7), head >> 7, -1)
-        member = one_hot_rows(bucket, BLOCKS)
-        ahead = dot_nn(spread(member, 1.0), before)
-        rank[:, cols] = jnp.sum(jnp.where(member, ahead + carry, 0.0), axis=0, keepdims=True)
-        return carry + jnp.sum(jnp.where(member, 1.0, 0.0), axis=1, keepdims=True)
-
-    total = lax.fori_loop(0, INNER // width, scan, jnp.zeros((BLOCKS, 1), F32))
-    add_degree(ends[0:1, INNER:], cond[:, INNER:])
-    deg = degree[0:32, :] + degree[32:64, :] + degree[64:96, :]
+        nodes, values = [], []
+        for i in range(SCANS):
+            cols = pl.ds(pl.multiple_of((SCANS * step + i) * width, width), width)
+            head = ends[0:1, cols]
+            tail = ends[1:2, cols]
+            value = cond[:, cols]
+            nodes += [head, tail]
+            values += [value, value]
+            bucket = jnp.where((head >> 7) == (tail >> 7), head >> 7, -1)
+            member = one_hot_rows(bucket, BLOCKS)
+            ahead = dot_nn(spread(member, 1.0), before)
+            rank[:, cols] = jnp.sum(jnp.where(member, ahead + carry, 0.0), axis=0, keepdims=True)
+            carry = carry + jnp.sum(jnp.where(member, 1.0, 0.0), axis=1, keepdims=True)
+        add_degree(nodes, values)
+        return carry
+
+    total = lax.fori_loop(0, INNER // width // SCANS, scan, jnp.zeros((BLOCKS, 1), F32))
+    add_degree([ends[0:1, INNER:]], [cond[:, INNER:]])
+    deg = degree[0:32, :] + degree[32:64, :]
     block_id = lax.broadcasted_iota(I32, (BLOCKS, TILE), 0)
     for j in range(SHOWN):
         deg = deg + jnp.where(block_id == shown[j], arrived[j : j + 1, :], 0.0)
@@ -156,7 +165,7 @@
         order = rank[:, cols].astype(I32)
         chunk = jnp.where(inside, base.astype(I32) + (order >> 7), -1)
         at_chunk = one_hot_rows(chunk, CHUNKS)
-        values = ((head & 127).astype(F32), (tail & 127).astype(F32)) + parts3(cond[:, cols])
+        values = ((head & 127).astype(F32), (tail & 127).astype(F32)) + parts2(cond[:, cols])
         stack = jnp.concatenate([spread(at_chunk, value) for value in values], axis=0)
         lanes = spread(one_hot_rows(order & 127, TILE), 1.0)
         sums[...] += dot_nt(stack, lanes)
@@ -169,71 +178,97 @@
     row_id = lax.broadcasted_iota(I32, (TILE, TILE), 0)
     lane_id = lax.broadcasted_iota(I32, (TILE, TILE), 1)
 
-    def fill(block, carry):
-        first = counts_smem[block, 0]
-        count = counts_smem[block + BLOCKS, 0]
-
-        def add_chunk(index, acc):
-            row = first + index
-            head = packed[pl.ds(row, 1), :].astype(I32)
-            tail = packed[pl.ds(row + CHUNKS, 1), :].astype(I32)
-            at_head = row_id == head
-            at_tail = row_id == tail
-            left = jnp.concatenate([spread(at_head, 1.0), spread(at_tail, 1.0)], axis=1)
-            for k in range(3):
-                value = packed[pl.ds(row + (2 + k) * CHUNKS, 1), :]
-                right = jnp.concatenate([spread(at_tail, value), spread(at_head, value)], axis=1)
-                acc = acc + dot_nt(left, right)
-            return acc
-
-        acc = lax.fori_loop(0, count, add_chunk, jnp.zeros((TILE, TILE), F32))
-        table[block] = jnp.where(row_id == lane_id, degree_out[pl.ds(block, 1), :], -acc)
+    def chunk_of(row, live):
+        head = packed[pl.ds(row, 1), :].astype(I32)
+        tail = packed[pl.ds(row + CHUNKS, 1), :].astype(I32)
+        at_head = row_id == head
+        at_tail = row_id == tail
+        left = jnp.concatenate([spread(at_head, 1.0), spread(at_tail, 1.0)], axis=1)
+        right = []
+        for k in range(2):
+            value = packed[pl.ds(row + (2 + k) * CHUNKS, 1), :] * live
+            right.append(jnp.concatenate([spread(at_tail, value), spread(at_head, value)], axis=1))
+        both = dot_nt(left, jnp.concatenate(right, axis=0))
+        return both[:, 0:TILE] + both[:, TILE:]
+
+    def fill(step, carry):
+        filled = []
+        for i in range(FOUR):
+            block = step * FOUR + i
+            live = jnp.where(counts_smem[block + BLOCKS, 0] > 0, 1.0, 0.0)
+            off = chunk_of(counts_smem[block, 0], live)
+            filled.append(jnp.where(row_id == lane_id, degree_out[pl.ds(block, 1), :], -off))
+        for i in range(FOUR):
+            table[pl.ds(pl.multiple_of((step * FOUR + i) * TILE, TILE), TILE), :] = filled[i]
         return carry
 
-    lax.fori_loop(0, BLOCKS, fill, 0)
+    lax.fori_loop(0, BLOCKS // FOUR, fill, 0)
+
+    def refill(block, carry):
+        rows = pl.ds(pl.multiple_of(block * TILE, TILE), TILE)
+
+        def more(index, inner):
+            table[rows, :] = table[rows, :] - chunk_of(counts_smem[block, 0] + index, 1.0)
+            return inner
+
+        lax.fori_loop(1, counts_smem[block + BLOCKS, 0], more, 0)
+        return carry
+
+    lax.fori_loop(0, BLOCKS, refill, 0)
 
     panel_lane = lax.broadcasted_iota(I32, (PANEL, TILE), 1)
     panel_row = lax.broadcasted_iota(I32, (PANEL, TILE), 0)
-    own_lane = panel_lane & (PANEL - 1)
     own_block = (row_id // PANEL) == (lane_id // PANEL)
+    lane_block = panel_lane & (PANEL - 1)
+    lane_group = panel_lane // PANEL
+
+    def replicated(x, group):
+        return jnp.take_along_axis(x, lane_block + group * PANEL, axis=1, mode="promise_in_bounds")
 
     def panel(index, carry):
         base = pl.multiple_of(index * PANEL, PANEL)
-        rows = pl.ds(base, PANEL)
-        olds = [table[b, rows, :] for b in range(BLOCKS)]
-        small = []
-        for g in range(BLOCKS // FOUR):
-            joined = jnp.zeros((PANEL, TILE), F32)
-            for i in range(FOUR):
-                turned = pltpu.roll(olds[g * FOUR + i], lax.rem(PANEL * i + TILE - base, TILE), 1)
-                joined = jnp.where((panel_lane // PANEL) == i, turned, joined)
-            small.append(joined)
-        for t in range(PANEL):
-            source = (panel_lane // PANEL) * PANEL + t
-            at_lane = own_lane == t
-            for g in range(BLOCKS // FOUR):
-                x = small[g]
-                column = jnp.take_along_axis(x, source, axis=1, mode="promise_in_bounds")
-                pivot = 1.0 / column[t : t + 1, :]
-                row = jnp.where(at_lane[0:1], pivot, x[t : t + 1, :] * pivot)
-                rest = jnp.where(at_lane, 0.0, x) - column * row
-                small[g] = jnp.where(panel_row == t, row, rest)
+        for b in range(BLOCKS):
+            old_rows[b * PANEL : (b + 1) * PANEL, :] = table[pl.ds(b * TILE + base, PANEL), :]
+        for i in range(8):
+            lines = [old_rows[pl.ds(8 * h + i, BLOCKS, stride=PANEL), :] for h in range(4)]
+            turned_rows[i] = jnp.concatenate(lines, axis=0).T
+        state = [turned_rows[i, pl.ds(base, PANEL), :] for i in range(8)]
+        for first in range(0, PANEL, 4):
+            coming = [replicated(state[(first + d) % 8], (first + d) // 8) for d in range(4)]
+            for d in range(4):
+                t = first + d
+                at_row = panel_row == t
+                now = coming[d]
+                pivot = 1.0 / now[t : t + 1, :]
+                new = jnp.where(at_row, pivot, now * pivot)
+                for e in range(d + 1, 4):
+                    x = coming[e]
+                    coming[e] = jnp.where(at_row, 0.0, x) - x[t : t + 1, :] * new
+                for i in range(8):
+                    x = state[i]
+                    rest = jnp.where(at_row, 0.0, x) - x[t : t + 1, :] * new
+                    state[i] = jnp.where(lane_group == t // 8, new, rest) if i == t % 8 else rest
+        for i in range(8):
+            back = jnp.concatenate([state[i]] * 4, axis=0).T
+            for h in range(4):
+                small[pl.ds(8 * h + i, BLOCKS, stride=PANEL), :] = back[PANEL * h : PANEL * h + PANEL, :]
         unit = jnp.where(panel_lane == panel_row + base, 1.0, 0.0)
         in_panel = (panel_lane >= base) & (panel_lane < base + PANEL)
         keep = ((lane_id >= base) & (lane_id < base + PANEL)) | ((row_id >= base) & (row_id < base + PANEL))
         zero = jnp.zeros((PANEL, TILE), BF16)
         for g in range(BLOCKS // FOUR):
-            diagonal = jnp.where(own_block, jnp.concatenate([small[g]] * FOUR, axis=0), 0.0)
-            members = [jnp.where(in_panel, unit, olds[g * FOUR + i]) for i in range(FOUR)]
+            span = slice(TILE * g, TILE * g + TILE)
+            diagonal = jnp.where(own_block, small[span, :], 0.0)
+            members = [jnp.where(in_panel, unit, old_rows[TILE * g + PANEL * i : TILE * g + PANEL * i + PANEL, :]) for i in range(FOUR)]
             stack = jnp.concatenate(members, axis=0)
-            dh, dm, dl = [part.astype(BF16) for part in parts3(diagonal)]
-            sh, sm, sl = [part.astype(BF16) for part in parts3(stack)]
-            fresh = dot_nn(jnp.concatenate([dh, dm], axis=1), jnp.concatenate([sh, sm], axis=0))
-            fresh = fresh + dot_nn(jnp.concatenate([dh, dm], axis=1), jnp.concatenate([sm, sh], axis=0))
-            fresh = fresh + dot_nn(jnp.concatenate([dh, dl], axis=1), jnp.concatenate([sl, sh], axis=0))
-            turned = jnp.where(row_id < base + PANEL, -stack.T, stack.T)
-            th, tm, tl = [part.astype(BF16) for part in parts3(turned)]
-            fh, fm, fl = [part.astype(BF16) for part in parts3(fresh)]
+            dh, dm = [part.astype(BF16) for part in parts2(diagonal)]
+            sh, sm = [part.astype(BF16) for part in parts2(stack)]
+            left = jnp.concatenate([dh, dm], axis=1)
+            fresh = dot_nn(left, jnp.concatenate([sh, sm], axis=0)) + dot_nn(left, jnp.concatenate([sm, sh], axis=0))
+            turned = stack.T
+            turned = jnp.where(row_id < base + PANEL, -turned, turned)
+            th, tm = [part.astype(BF16) for part in parts2(turned)]
+            fh, fm = [part.astype(BF16) for part in parts2(fresh)]
 
             def across(value):
                 lines = []
@@ -243,19 +278,18 @@
                     lines.append(jnp.concatenate(cells, axis=1))
                 return jnp.concatenate(lines, axis=0)
 
-            ah, am, al = across(fh), across(fm), across(fl)
-            update = dot_nn(jnp.concatenate([th, tm], axis=1), jnp.concatenate([ah, am], axis=0))
-            update = update + dot_nn(jnp.concatenate([th, tm], axis=1), jnp.concatenate([am, ah], axis=0))
-            update = update + dot_nn(jnp.concatenate([th, tl], axis=1), jnp.concatenate([al, ah], axis=0))
+            ah, am = across(fh), across(fm)
+            left = jnp.concatenate([th, tm], axis=1)
+            update = dot_nn(left, jnp.concatenate([ah, am], axis=0)) + dot_nn(left, jnp.concatenate([am, ah], axis=0))
             for i in range(FOUR):
-                b = g * FOUR + i
-                table[b] = jnp.where(keep, 0.0, table[b]) - update[:, TILE * i : TILE * i + TILE]
+                rows = slice((g * FOUR + i) * TILE, (g * FOUR + i + 1) * TILE)
+                table[rows, :] = jnp.where(keep, 0.0, table[rows, :]) - update[:, TILE * i : TILE * i + TILE]
         return carry
 
     lax.fori_loop(0, TILE // PANEL, panel, 0)
 
     def finish(block, carry):
-        inverse[block] = table[block].astype(BF16)
+        inverse[block] = table[pl.ds(pl.multiple_of(block * TILE, TILE), TILE), :].astype(BF16)
         return carry
 
     lax.fori_loop(0, BLOCKS, finish, 0)
@@ -504,6 +538,29 @@
     return [pl.BlockSpec(memory_space=pltpu.SMEM)] * count
 
 
+def setup_call(ends, cond, mask, shown, arrived):
+    return pl.pallas_call(
+        setup_kernel,
+        out_shape=(jax.ShapeDtypeStruct((BLOCKS, TILE, TILE), BF16), jax.ShapeDtypeStruct((BLOCKS, TILE), F32)),
+        in_specs=vmem(3) + smem(1) + vmem(1),
+        out_specs=tuple(vmem(2)),
+        scratch_shapes=[
+            pltpu.VMEM((NODES, TILE), F32),
+            pltpu.VMEM((1, INNER), F32),
+            pltpu.VMEM((64, TILE), F32),
+            pltpu.VMEM((4 * CHUNKS, TILE), F32),
+            pltpu.VMEM((4 * CHUNKS, TILE), F32),
+            pltpu.VMEM((64, TILE), I32),
+            pltpu.VMEM((BLOCKS * PANEL, TILE), F32),
+            pltpu.VMEM((8, TILE, TILE), F32),
+            pltpu.VMEM((BLOCKS * PANEL, TILE), F32),
+            pltpu.SMEM((64, TILE), I32),
+            pltpu.SemaphoreType.DMA,
+        ],
+        name="inverses",
+    )(ends, cond, mask, shown, arrived)
+
+
 def per_device(sizes, inflow, mask, ends, live, shown, radius, length):
     parts, depth_z, planes, reps = sizes
     mask = mask.reshape(BLOCKS, TILE)
@@ -517,23 +574,7 @@
         compiler_params=pltpu.CompilerParams(collective_id=0, has_side_effects=True),
         name="conductances",
     )(ends, radius.reshape(1, SEGS), length.reshape(1, SEGS), live)
-    inverse, degree = pl.pallas_call(
-        setup_kernel,
-        out_shape=(jax.ShapeDtypeStruct((BLOCKS, TILE, TILE), BF16), jax.ShapeDtypeStruct((BLOCKS, TILE), F32)),
-        in_specs=vmem(3) + smem(1) + vmem(1),
-        out_specs=tuple(vmem(2)),
-        scratch_shapes=[
-            pltpu.VMEM((BLOCKS, TILE, TILE), F32),
-            pltpu.VMEM((1, INNER), F32),
-            pltpu.VMEM((96, TILE), F32),
-            pltpu.VMEM((5 * CHUNKS, TILE), F32),
-            pltpu.VMEM((5 * CHUNKS, TILE), F32),
-            pltpu.VMEM((64, TILE), I32),
-            pltpu.SMEM((64, TILE), I32),
-            dma,
-        ],
-        name="inverses",
-    )(ends, cond, mask, shown, arrived)
+    inverse, degree = setup_call(ends, cond, mask, shown, arrived)
     rows = 8 * BLOCKS
     back = 8 * SHOWN
     pressure, mean = pl.pallas_call(

time: 100 us -> 79.7 us (0.80)
  Pallas kernels: 95.3 us -> 74.6 us
    pallas_call x1, Pallas kernels: 49 us -> 28.3 us  [setup_call(): pl.pallas_call(setup_kernel, out_shape=(jax.ShapeDtypeStruct((BLOCKS, TIL...]
where the time goes in v3:
time: 79.7 us; the launch traced here: 79.4 us
  Pallas kernels  74.6 us (94%)
  local copies, waits for them, and re-layouts  3.49 us (4%)
  between operations  1.32 us (2%)
    pallas_call x1, Pallas kernels, per_device(): pl.pallas_call(functools.partial(solve_kernel, sizes), out_shape=(jax.Sha...  34.9 us
    pallas_call x1, Pallas kernels, setup_call(): pl.pallas_call(setup_kernel, out_shape=(jax.ShapeDtypeStruct((BLOCKS, TIL...  28.3 us
    pallas_call x1, Pallas kernels, per_device(): pl.pallas_call(functools.partial(head_kernel, parts), out_shape=(jax.Shap...  11.4 us
    unnamed x6, local copies, waits for them, and re-layouts  2.83 us

profile of v3, /device:TPU:1, one launch (start us, length us, event | category | flops | bytes accessed | tf_op | source)
XLA Modules:
  0.0 79.4 jit_solution(2102374072874803799)
XLA Ops:
  1.3 0.0 copy-start.1
  1.3 0.6 copy-done.1
  1.9 0.7 broadcast_in_dim.2.shown
  2.6 11.4 %conductances.1 = (f32[1,7168]{1,0:T(1,128)}, f32[8,128]{1,0:T(8,128)}) custom-call(s32[2,7168]{1,0:T(2,128)} %ends.5, f32[1,7168]{1,0:T(1,128)} %bitcast.6, f32[1,7168]{1,0:T(1,128)} %bitcast.7, s32[1]{0:T(128)S(6)} %copy.11.live), custom_call_target="tpu_custom_call" | custom-call | tf_op jit(solution)/shard_map/conductances/pallas_call | solution.py:568
  14.0 28.3 %inverses.1 = (bf16[32,128,128]{2,1,0:T(8,128)(2,1)}, f32[32,128]{1,0:T(8,128)}) custom-call(s32[2,7168]{1,0:T(2,128)} %ends.5, f32[1,7168]{1,0:T(1,128)} %get-tuple-element.8.cond, s32[32,128]{1,0:T(8,128)} %bitcast.4, s32[8]{0:T(128)} %shown.1, f32[8,128]{1,0:T(8,128)} %get-tuple-element.9.arrived), custom_call_target="tpu_custom_call" | custom-call | tf_op jit(solution)/shard_map/inverses/pallas_call | solution.py:542
  42.3 34.9 %gradients.1 = (f32[8,4096]{1,0:T(8,128)}, f32[32,128]{1,0:T(8,128)}) custom-call(f32[8,4096]{1,0:T(8,128)} %inflow.1, s32[32,128]{1,0:T(8,128)} %bitcast.5, s32[2,7168]{1,0:T(2,128)} %ends.5, f32[1,7168]{1,0:T(1,128)} %get-tuple-element.8.cond, f32[32,128]{1,0:T(8,128)} %get-tuple-element.10.degree, bf16[32,128,128]{2,1,0:T(8,128)(2,1)} %get-tuple-element.11.inverse, ...), custom_call_target="tpu_custom_call" | custom-call | tf_op jit(solution)/shard_map/gradients/pallas_call | solution.py:580
  77.3 0.0 copy-start
  77.3 1.6 %copy.12 = f32[8,4096]{1,0:T(8,128)} copy(f32[8,4096]{1,0:T(8,128)} %get-tuple-element.16) | data formatting | bytes 262144
  78.8 0.0 copy-done
  78.8 0.6 copy.13
Async XLA Ops:
  1.3 0.7 copy-start.1
  77.3 1.6 %copy-start = (f32[32,128]{1,0:T(8,128)S(1)}, f32[32,128]{1,0:T(8,128)}, u32[]{:S(2)}) copy-start(f32[32,128]{1,0:T(8,128)} %get-tuple-element.13) | copy-start | bytes 49156

commit v4 on v3

--- a/solution.py
+++ b/solution.py
@@ -22,9 +22,10 @@
 SHOWN = 8
 CHUNKS = 80
 PANEL = 32
+PITCH = 40
 FOUR = 4
 UNROLL = 4
-SCANS = 2
+SCANS = 4
 
 leak_rate = 0.05
 inflow_weight = 20.0
@@ -57,6 +58,11 @@
 def one_hot_rows(row, count):
     ids = lax.broadcasted_iota(I32, (count, row.shape[1]), 0)
     return ids == row
+
+
+def one_hot_lanes(row, count):
+    ids = lax.broadcasted_iota(I32, (count, row.shape[1]), 0).astype(F32).astype(BF16)
+    return jnp.where(ids == row.astype(F32).astype(BF16), jnp.ones((), BF16), jnp.zeros((), BF16))
 
 
 def spread(mask, value):
@@ -153,7 +159,7 @@
     to_scalar = pltpu.make_async_copy(counts, counts_smem, sem)
     to_scalar.start()
     start_column = start[:, 0:1]
-    wide = 512
+    wide = 1024
 
     def compact(step, carry):
         cols = pl.ds(pl.multiple_of(step * wide, wide), wide)
@@ -228,9 +234,9 @@
     def panel(index, carry):
         base = pl.multiple_of(index * PANEL, PANEL)
         for b in range(BLOCKS):
-            old_rows[b * PANEL : (b + 1) * PANEL, :] = table[pl.ds(b * TILE + base, PANEL), :]
+            old_rows[b * PITCH : b * PITCH + PANEL, :] = table[pl.ds(b * TILE + base, PANEL), :]
         for i in range(8):
-            lines = [old_rows[pl.ds(8 * h + i, BLOCKS, stride=PANEL), :] for h in range(4)]
+            lines = [old_rows[pl.ds(8 * h + i, BLOCKS, stride=PITCH), :] for h in range(4)]
             turned_rows[i] = jnp.concatenate(lines, axis=0).T
         state = [turned_rows[i, pl.ds(base, PANEL), :] for i in range(8)]
         for first in range(0, PANEL, 4):
@@ -251,48 +257,39 @@
         for i in range(8):
             back = jnp.concatenate([state[i]] * 4, axis=0).T
             for h in range(4):
-                small[pl.ds(8 * h + i, BLOCKS, stride=PANEL), :] = back[PANEL * h : PANEL * h + PANEL, :]
+                small[pl.ds(8 * h + i, BLOCKS, stride=PITCH), :] = back[PANEL * h : PANEL * h + PANEL, :]
         unit = jnp.where(panel_lane == panel_row + base, 1.0, 0.0)
         in_panel = (panel_lane >= base) & (panel_lane < base + PANEL)
         keep = ((lane_id >= base) & (lane_id < base + PANEL)) | ((row_id >= base) & (row_id < base + PANEL))
-        zero = jnp.zeros((PANEL, TILE), BF16)
         for g in range(BLOCKS // FOUR):
-            span = slice(TILE * g, TILE * g + TILE)
-            diagonal = jnp.where(own_block, small[span, :], 0.0)
-            members = [jnp.where(in_panel, unit, old_rows[TILE * g + PANEL * i : TILE * g + PANEL * i + PANEL, :]) for i in range(FOUR)]
+            starts = [PITCH * (g * FOUR + i) for i in range(FOUR)]
+            diagonal = jnp.where(own_block, jnp.concatenate([small[at : at + PANEL, :] for at in starts], axis=0), 0.0)
+            members = [jnp.where(in_panel, unit, old_rows[at : at + PANEL, :]) for at in starts]
             stack = jnp.concatenate(members, axis=0)
             dh, dm = [part.astype(BF16) for part in parts2(diagonal)]
             sh, sm = [part.astype(BF16) for part in parts2(stack)]
-            left = jnp.concatenate([dh, dm], axis=1)
-            fresh = dot_nn(left, jnp.concatenate([sh, sm], axis=0)) + dot_nn(left, jnp.concatenate([sm, sh], axis=0))
+            def crossed(high, low):
+                return jnp.concatenate([jnp.concatenate([high, low], axis=1), jnp.concatenate([low, high], axis=1)], axis=0)
+
+            fresh = dot_nn(jnp.concatenate([dh, dm], axis=1), crossed(sh, sm))
+            fresh = fresh[:, 0:TILE] + fresh[:, TILE:]
             turned = stack.T
             turned = jnp.where(row_id < base + PANEL, -turned, turned)
-            th, tm = [part.astype(BF16) for part in parts2(turned)]
+            parts = [part.astype(BF16) for part in parts2(turned)]
             fh, fm = [part.astype(BF16) for part in parts2(fresh)]
-
-            def across(value):
-                lines = []
-                for i in range(FOUR):
-                    cells = [zero] * FOUR
-                    cells[i] = value[PANEL * i : PANEL * i + PANEL, :]
-                    lines.append(jnp.concatenate(cells, axis=1))
-                return jnp.concatenate(lines, axis=0)
-
-            ah, am = across(fh), across(fm)
-            left = jnp.concatenate([th, tm], axis=1)
-            update = dot_nn(left, jnp.concatenate([ah, am], axis=0)) + dot_nn(left, jnp.concatenate([am, ah], axis=0))
+            none = jnp.zeros((TILE, TILE), BF16)
+            left = [jnp.concatenate([jnp.where((lane_id // PANEL) == i, part, none) for part in parts], axis=1) for i in range(FOUR)]
+            update = dot_nn(jnp.concatenate(left, axis=0), crossed(fh, fm))
+            update = update[:, 0:TILE] + update[:, TILE:]
             for i in range(FOUR):
                 rows = slice((g * FOUR + i) * TILE, (g * FOUR + i + 1) * TILE)
-                table[rows, :] = jnp.where(keep, 0.0, table[rows, :]) - update[:, TILE * i : TILE * i + TILE]
+                table[rows, :] = jnp.where(keep, 0.0, table[rows, :]) - update[TILE * i : TILE * i + TILE, :]
         return carry
 
     lax.fori_loop(0, TILE // PANEL, panel, 0)
 
-    def finish(block, carry):
-        inverse[block] = table[pl.ds(pl.multiple_of(block * TILE, TILE), TILE), :].astype(BF16)
-        return carry
-
-    lax.fori_loop(0, BLOCKS, finish, 0)
+    for block in range(BLOCKS):
+        inverse[block] = table[block * TILE : (block + 1) * TILE, :].astype(BF16)
 
 
 def solve_kernel(
@@ -334,7 +331,7 @@
         for side in range(2):
             node = ends[side : side + 1, cols]
             into = pl.ds(pl.multiple_of(side * SEGS + step * wide, wide), wide)
-            table[:, into] = spread(one_hot_rows(node & 255, 256), 1.0)
+            table[:, into] = one_hot_lanes(node & 255, 256)
             owner8[:, into] = jnp.broadcast_to(node >> 8, (8, wide))
         return carry
 
@@ -351,12 +348,14 @@
             target[8 * q : 8 * q + 16, :] = jnp.concatenate(highs, axis=1).astype(BF16)
             target[rows + 8 * q : rows + 8 * q + 16, :] = jnp.concatenate(lows, axis=1).astype(BF16)
 
-    def gather(source, cols, pairs):
-        full = dot_nn(source[...], table[:, cols])
+    def gather(source, cols, pairs, both):
+        full = dot_nn(source[...] if both else source[0 : 8 * pairs, :], table[:, cols])
         owner = owner8[:, cols]
         result = jnp.zeros((8, wide), F32)
         for q in range(pairs):
-            value = full[8 * q : 8 * q + 8, :] + full[8 * (q + pairs) : 8 * (q + pairs) + 8, :]
+            value = full[8 * q : 8 * q + 8, :]
+            if both:
+                value = value + full[8 * (q + pairs) : 8 * (q + pairs) + 8, :]
             result = jnp.where(owner == q, value, result)
         return result
 
@@ -384,7 +383,10 @@
     def precondition(k):
         for b in range(BLOCKS):
             field = residual[8 * b : 8 * b + 8, :].astype(BF16)
-            basis[k, 8 * b : 8 * b + 8, :] = dot_nn(field, inverse[b])
+            value = dot_nn(field, inverse[b])
+            if k == 1:
+                value = value.astype(BF16).astype(F32)
+            basis[k, 8 * b : 8 * b + 8, :] = value
 
     for b in range(BLOCKS):
         weight = inflow_weight * mask[b : b + 1, :].astype(F32)
@@ -409,7 +411,7 @@
     for k in range(3):
         split_into(pair, lambda b: basis[k, 8 * b : 8 * b + 8, :], pairs_all)
         for j in range(SHOWN):
-            wanted = jnp.broadcast_to(shown[j : j + 1, :], (8, TILE))
+            wanted = jnp.full((8, TILE), shown[j], I32)
             tile = jnp.zeros((8, TILE), F32)
             for b in range(BLOCKS):
                 tile = jnp.where(wanted == b, basis[k, 8 * b : 8 * b + 8, :], tile)
@@ -425,7 +427,7 @@
         if k < 2:
             hcols = [head_cols(junc_first + step) for step in range(junc_steps)]
             tcols = [tail_cols(junc_first + step) for step in range(junc_steps)]
-            back_out[...] = scatter([cond8[:, at] * gather(pair, at, pairs_all) for at in hcols], tcols, pairs_shown)
+            back_out[...] = scatter([cond8[:, at] * gather(pair, at, pairs_all, k == 0) for at in hcols], tcols, pairs_shown)
             for j in range(SHOWN):
                 back_src[k, 8 * j : 8 * j + 8, :] = tile_of(back_out, j, pairs_shown)
             backward = pltpu.make_async_remote_copy(
@@ -440,7 +442,7 @@
                 for i in range(UNROLL):
                     h, t = head_cols(UNROLL * step + i), tail_cols(UNROLL * step + i)
                     weight = cond8[:, h]
-                    values += [weight * gather(pair, t, pairs_all), weight * gather(pair, h, pairs_all)]
+                    values += [weight * gather(pair, t, pairs_all, k == 0), weight * gather(pair, h, pairs_all, k == 0)]
                     cols += [h, t]
                 out[...] += scatter(values, cols, pairs_all)
                 return carry
@@ -448,12 +450,12 @@
             lax.fori_loop(0, INNER // wide // UNROLL, inner, 0)
             forward.wait()
             split_into(upper_pair, lambda j: fwd_in[k, 8 * j : 8 * j + 8, :], pairs_shown)
-            out[...] += scatter([cond8[:, h] * gather(upper_pair, t, pairs_shown) for h, t in zip(hcols, tcols)], hcols, pairs_all)
+            out[...] += scatter([cond8[:, h] * gather(upper_pair, t, pairs_shown, k == 0) for h, t in zip(hcols, tcols)], hcols, pairs_all)
             backward.wait()
             for b in range(BLOCKS):
                 acc = tile_of(out, b, pairs_all)
                 for j in range(SHOWN):
-                    acc = acc + jnp.where(jnp.broadcast_to(shown[j : j + 1, :], (8, TILE)) == b, back_in[k, 8 * j : 8 * j + 8, :], 0.0)
+                    acc = acc + jnp.where(jnp.full((8, TILE), shown[j], I32) == b, back_in[k, 8 * j : 8 * j + 8, :], 0.0)
                 image = degree[b : b + 1, :] * basis[k, 8 * b : 8 * b + 8, :] - acc
                 images[k, 8 * b : 8 * b + 8, :] = image
                 residual[8 * b : 8 * b + 8, :] = residual[8 * b : 8 * b + 8, :] - image
@@ -464,15 +466,15 @@
             def quadratic(step, carry):
                 for i in range(UNROLL):
                     h, t = head_cols(UNROLL * step + i), tail_cols(UNROLL * step + i)
-                    carry = carry + cond8[:, h] * gather(pair, h, pairs_all) * gather(pair, t, pairs_all)
+                    carry = carry + cond8[:, h] * gather(pair, h, pairs_all, k == 0) * gather(pair, t, pairs_all, k == 0)
                 return carry
 
             crossed = lax.fori_loop(0, INNER // wide // UNROLL, quadratic, jnp.zeros((8, wide), F32))
-            ahead = [cond8[:, head_cols(junc_first + step)] * gather(pair, head_cols(junc_first + step), pairs_all) for step in range(junc_steps)]
+            ahead = [cond8[:, head_cols(junc_first + step)] * gather(pair, head_cols(junc_first + step), pairs_all, k == 0) for step in range(junc_steps)]
             forward.wait()
             split_into(upper_pair, lambda j: fwd_in[k, 8 * j : 8 * j + 8, :], pairs_shown)
             for step in range(junc_steps):
-                crossed = crossed + ahead[step] * gather(upper_pair, tail_cols(junc_first + step), pairs_shown)
+                crossed = crossed + ahead[step] * gather(upper_pair, tail_cols(junc_first + step), pairs_shown, k == 0)
             square = total_of(2, lambda b: degree[b : b + 1, :] * basis[2, 8 * b : 8 * b + 8, :])
             square = square - 2.0 * jnp.sum(crossed, axis=1, keepdims=True)
             moments = jnp.where(lane == 5, square, moments)
@@ -551,9 +553,9 @@
             pltpu.VMEM((4 * CHUNKS, TILE), F32),
             pltpu.VMEM((4 * CHUNKS, TILE), F32),
             pltpu.VMEM((64, TILE), I32),
-            pltpu.VMEM((BLOCKS * PANEL, TILE), F32),
+            pltpu.VMEM((BLOCKS * PITCH, TILE), F32),
             pltpu.VMEM((8, TILE, TILE), F32),
-            pltpu.VMEM((BLOCKS * PANEL, TILE), F32),
+            pltpu.VMEM((BLOCKS * PITCH, TILE), F32),
             pltpu.SMEM((64, TILE), I32),
             pltpu.SemaphoreType.DMA,
         ],
@@ -580,7 +582,7 @@
     pressure, mean = pl.pallas_call(
         functools.partial(solve_kernel, sizes),
         out_shape=(jax.ShapeDtypeStruct((8, NODES), F32), jax.ShapeDtypeStruct((BLOCKS, TILE), F32)),
-        in_specs=vmem(7),
+        in_specs=vmem(6) + smem(1),
         out_specs=tuple(vmem(2)),
         scratch_shapes=[
             pltpu.VMEM((2 * TILE, 2 * SEGS), BF16),
@@ -605,7 +607,7 @@
         ],
         compiler_params=pltpu.CompilerParams(collective_id=1, has_side_effects=True),
         name="gradients",
-    )(inflow, mask, ends, cond, degree, inverse, jnp.broadcast_to(shown[:, None], (SHOWN, TILE)))
+    )(inflow, mask, ends, cond, degree, inverse, shown)
     return pressure, mean.reshape(NODES)
 
 

time: 79.7 us -> 70.7 us (0.89)
  Pallas kernels: 74.6 us -> 67 us
  local copies, waits for them, and re-layouts: 3.49 us -> 2.18 us
    pallas_call x1, Pallas kernels: 28.3 us -> 21.9 us  [setup_call(): pl.pallas_call(setup_kernel, out_shape=(jax.ShapeDtypeStruct((BLOCKS, TIL...]
    pallas_call x1, Pallas kernels: 34.9 us -> 33.6 us  [per_device(): pl.pallas_call(functools.partial(solve_kernel, sizes), out_shape=(jax.Sha...]
    unnamed x6 -> x4, local copies, waits for them, and re-layouts: 2.83 us -> 2.18 us
where the time goes in v4:
time: 70.7 us; the launch traced here: 70.5 us
  Pallas kernels  67 us (95%)
  local copies, waits for them, and re-layouts  2.18 us (3%)
  between operations  1.31 us (2%)
    pallas_call x1, Pallas kernels, per_device(): pl.pallas_call(functools.partial(solve_kernel, sizes), out_shape=(jax.Sha...  33.6 us
    pallas_call x1, Pallas kernels, setup_call(): pl.pallas_call(setup_kernel, out_shape=(jax.ShapeDtypeStruct((BLOCKS, TIL...  21.9 us
    pallas_call x1, Pallas kernels, per_device(): pl.pallas_call(functools.partial(head_kernel, parts), out_shape=(jax.Shap...  11.5 us
    unnamed x4, local copies, waits for them, and re-layouts  2.18 us

profile of v4, /device:TPU:1, one launch (start us, length us, event | category | flops | bytes accessed | tf_op | source)
XLA Modules:
  0.0 70.5 jit_solution(17038423834887692801)
XLA Ops:
  1.3 11.5 %conductances.1 = (f32[1,7168]{1,0:T(1,128)}, f32[8,128]{1,0:T(8,128)}) custom-call(s32[2,7168]{1,0:T(2,128)} %ends.5, f32[1,7168]{1,0:T(1,128)} %bitcast.6, f32[1,7168]{1,0:T(1,128)} %bitcast.7, s32[1]{0:T(128)S(6)} %copy.11.live), custom_call_target="tpu_custom_call" | custom-call | tf_op jit(solution)/shard_map/conductances/pallas_call | solution.py:570
  12.8 21.9 %inverses.1 = (bf16[32,128,128]{2,1,0:T(8,128)(2,1)}, f32[32,128]{1,0:T(8,128)}) custom-call(s32[2,7168]{1,0:T(2,128)} %ends.5, f32[1,7168]{1,0:T(1,128)} %get-tuple-element.8.cond, s32[32,128]{1,0:T(8,128)} %bitcast.4, s32[8]{0:T(128)} %shown.3, f32[8,128]{1,0:T(8,128)} %get-tuple-element.9.arrived), custom_call_target="tpu_custom_call" | custom-call | tf_op jit(solution)/shard_map/inverses/pallas_call | solution.py:544
  34.7 33.6 %gradients.1 = (f32[8,4096]{1,0:T(8,128)}, f32[32,128]{1,0:T(8,128)}) custom-call(f32[8,4096]{1,0:T(8,128)} %inflow.1, s32[32,128]{1,0:T(8,128)} %bitcast.5, s32[2,7168]{1,0:T(2,128)} %ends.5, f32[1,7168]{1,0:T(1,128)} %get-tuple-element.8.cond, f32[32,128]{1,0:T(8,128)} %get-tuple-element.10.degree, bf16[32,128,128]{2,1,0:T(8,128)(2,1)} %get-tuple-element.11.inverse, ...), custom_call_target="tpu_custom_call" | custom-call | tf_op jit(solution)/shard_map/gradients/pallas_call | solution.py:582
  68.3 0.0 copy-start
  68.3 1.6 %copy.12 = f32[8,4096]{1,0:T(8,128)} copy(f32[8,4096]{1,0:T(8,128)} %get-tuple-element.16) | data formatting | bytes 262144
  69.9 0.0 copy-done
  69.9 0.6 copy.13
Async XLA Ops:
  68.3 1.6 %copy-start = (f32[32,128]{1,0:T(8,128)S(1)}, f32[32,128]{1,0:T(8,128)}, u32[]{:S(2)}) copy-start(f32[32,128]{1,0:T(8,128)} %get-tuple-element.13) | copy-start | bytes 49156

commit v5 on v4

--- a/solution.py
+++ b/solution.py
@@ -24,8 +24,9 @@
 PANEL = 32
 PITCH = 40
 FOUR = 4
-UNROLL = 4
+UNROLL = 8
 SCANS = 4
+FILLS = 8
 
 leak_rate = 0.05
 inflow_weight = 20.0
@@ -122,7 +123,7 @@
         for node, value in zip(nodes, values):
             owner = one_hot_rows(node >> 7, BLOCKS)
             stacks.append(jnp.concatenate([jnp.where(owner, part, 0.0) for part in parts2(value)], axis=0).astype(BF16))
-            lanes.append(spread(one_hot_rows(node & 127, TILE), 1.0))
+            lanes.append(one_hot_lanes(node & 127, TILE))
         degree[...] += dot_nt(jnp.concatenate(stacks, axis=1), jnp.concatenate(lanes, axis=1))
 
     def scan(step, carry):
@@ -156,6 +157,7 @@
     start = dot_nn(jnp.where(below, 1.0, 0.0).astype(BF16), chunks.astype(BF16))
     counts[0:32, :] = start.astype(I32)
     counts[32:64, :] = chunks.astype(I32)
+    counts[64:72, :] = jnp.broadcast_to(jnp.max(chunks, axis=0, keepdims=True), (8, TILE)).astype(I32)
     to_scalar = pltpu.make_async_copy(counts, counts_smem, sem)
     to_scalar.start()
     start_column = start[:, 0:1]
@@ -173,7 +175,7 @@
         at_chunk = one_hot_rows(chunk, CHUNKS)
         values = ((head & 127).astype(F32), (tail & 127).astype(F32)) + parts2(cond[:, cols])
         stack = jnp.concatenate([spread(at_chunk, value) for value in values], axis=0)
-        lanes = spread(one_hot_rows(order & 127, TILE), 1.0)
+        lanes = one_hot_lanes(order & 127, TILE)
         sums[...] += dot_nt(stack, lanes)
         return carry
 
@@ -199,16 +201,16 @@
 
     def fill(step, carry):
         filled = []
-        for i in range(FOUR):
-            block = step * FOUR + i
+        for i in range(FILLS):
+            block = step * FILLS + i
             live = jnp.where(counts_smem[block + BLOCKS, 0] > 0, 1.0, 0.0)
             off = chunk_of(counts_smem[block, 0], live)
             filled.append(jnp.where(row_id == lane_id, degree_out[pl.ds(block, 1), :], -off))
-        for i in range(FOUR):
-            table[pl.ds(pl.multiple_of((step * FOUR + i) * TILE, TILE), TILE), :] = filled[i]
+        for i in range(FILLS):
+            table[pl.ds(pl.multiple_of((step * FILLS + i) * TILE, TILE), TILE), :] = filled[i]
         return carry
 
-    lax.fori_loop(0, BLOCKS // FOUR, fill, 0)
+    lax.fori_loop(0, BLOCKS // FILLS, fill, 0)
 
     def refill(block, carry):
         rows = pl.ds(pl.multiple_of(block * TILE, TILE), TILE)
@@ -220,7 +222,9 @@
         lax.fori_loop(1, counts_smem[block + BLOCKS, 0], more, 0)
         return carry
 
-    lax.fori_loop(0, BLOCKS, refill, 0)
+    @pl.when(counts_smem[64, 0] > 1)
+    def _():
+        lax.fori_loop(0, BLOCKS, refill, 0)
 
     panel_lane = lax.broadcasted_iota(I32, (PANEL, TILE), 1)
     panel_row = lax.broadcasted_iota(I32, (PANEL, TILE), 0)
@@ -335,7 +339,7 @@
             owner8[:, into] = jnp.broadcast_to(node >> 8, (8, wide))
         return carry
 
-    lax.fori_loop(0, SEGS // wide, make, 0)
+    lax.fori_loop(0, SEGS // wide, make, 0, unroll=4)
 
     def split_into(target, tile, pairs):
         rows = 8 * pairs
@@ -397,10 +401,10 @@
     moments = jnp.zeros((8, TILE), F32)
 
     def total_of(k, other):
-        acc = jnp.zeros((8, TILE), F32)
+        accs = [jnp.zeros((8, TILE), F32)] * 4
         for b in range(BLOCKS):
-            acc = acc + basis[k, 8 * b : 8 * b + 8, :] * other(b)
-        return jnp.sum(acc, axis=1, keepdims=True)
+            accs[b % 4] = accs[b % 4] + basis[k, 8 * b : 8 * b + 8, :] * other(b)
+        return jnp.sum((accs[0] + accs[1]) + (accs[2] + accs[3]), axis=1, keepdims=True)
 
     def right_side(b):
         weight = inflow_weight * mask[b : b + 1, :].astype(F32)
@@ -552,11 +556,11 @@
             pltpu.VMEM((64, TILE), F32),
             pltpu.VMEM((4 * CHUNKS, TILE), F32),
             pltpu.VMEM((4 * CHUNKS, TILE), F32),
-            pltpu.VMEM((64, TILE), I32),
+            pltpu.VMEM((72, TILE), I32),
             pltpu.VMEM((BLOCKS * PITCH, TILE), F32),
             pltpu.VMEM((8, TILE, TILE), F32),
             pltpu.VMEM((BLOCKS * PITCH, TILE), F32),
-            pltpu.SMEM((64, TILE), I32),
+            pltpu.SMEM((72, TILE), I32),
             pltpu.SemaphoreType.DMA,
         ],
         name="inverses",

time: 70.7 us -> 67.7 us (0.958)
  Pallas kernels: 67 us -> 63.7 us
    pallas_call x1, Pallas kernels: 33.6 us -> 31.6 us  [per_device(): pl.pallas_call(functools.partial(solve_kernel, sizes), out_shape=(jax.Sha...]
    pallas_call x1, Pallas kernels: 21.9 us -> 20.7 us  [setup_call(): pl.pallas_call(setup_kernel, out_shape=(jax.ShapeDtypeStruct((BLOCKS, TIL...]
where the time goes in v5:
time: 67.7 us; the launch traced here: 67.2 us
  Pallas kernels  63.7 us (94%)
  local copies, waits for them, and re-layouts  2.18 us (3%)
  between operations  1.31 us (2%)
    pallas_call x1, Pallas kernels, per_device(): pl.pallas_call(functools.partial(solve_kernel, sizes), out_shape=(jax.Sha...  31.6 us
    pallas_call x1, Pallas kernels, setup_call(): pl.pallas_call(setup_kernel, out_shape=(jax.ShapeDtypeStruct((BLOCKS, TIL...  20.7 us
    pallas_call x1, Pallas kernels, per_device(): pl.pallas_call(functools.partial(head_kernel, parts), out_shape=(jax.Shap...  11.5 us
    unnamed x4, local copies, waits for them, and re-layouts  2.18 us

profile of v5, /device:TPU:1, one launch (start us, length us, event | category | flops | bytes accessed | tf_op | source)
XLA Modules:
  0.0 67.2 jit_solution(3235457361710155975)
XLA Ops:
  1.3 11.5 %conductances.1 = (f32[1,7168]{1,0:T(1,128)}, f32[8,128]{1,0:T(8,128)}) custom-call(s32[2,7168]{1,0:T(2,128)} %ends.5, f32[1,7168]{1,0:T(1,128)} %bitcast.6, f32[1,7168]{1,0:T(1,128)} %bitcast.7, s32[1]{0:T(128)S(6)} %copy.11.live), custom_call_target="tpu_custom_call" | custom-call | tf_op jit(solution)/shard_map/conductances/pallas_call | solution.py:574
  12.8 20.7 %inverses.1 = (bf16[32,128,128]{2,1,0:T(8,128)(2,1)}, f32[32,128]{1,0:T(8,128)}) custom-call(s32[2,7168]{1,0:T(2,128)} %ends.5, f32[1,7168]{1,0:T(1,128)} %get-tuple-element.8.cond, s32[32,128]{1,0:T(8,128)} %bitcast.4, s32[8]{0:T(128)} %shown.3, f32[8,128]{1,0:T(8,128)} %get-tuple-element.9.arrived), custom_call_target="tpu_custom_call" | custom-call | tf_op jit(solution)/shard_map/inverses/pallas_call | solution.py:548
  33.4 31.6 %gradients.1 = (f32[8,4096]{1,0:T(8,128)}, f32[32,128]{1,0:T(8,128)}) custom-call(f32[8,4096]{1,0:T(8,128)} %inflow.1, s32[32,128]{1,0:T(8,128)} %bitcast.5, s32[2,7168]{1,0:T(2,128)} %ends.5, f32[1,7168]{1,0:T(1,128)} %get-tuple-element.8.cond, f32[32,128]{1,0:T(8,128)} %get-tuple-element.10.degree, bf16[32,128,128]{2,1,0:T(8,128)(2,1)} %get-tuple-element.11.inverse, ...), custom_call_target="tpu_custom_call" | custom-call | tf_op jit(solution)/shard_map/gradients/pallas_call | solution.py:586
  65.0 0.0 copy-start
  65.0 1.6 %copy.12 = f32[8,4096]{1,0:T(8,128)} copy(f32[8,4096]{1,0:T(8,128)} %get-tuple-element.16) | data formatting | bytes 262144
  66.6 0.0 copy-done
  66.6 0.6 copy.13
Async XLA Ops:
  65.0 1.6 %copy-start = (f32[32,128]{1,0:T(8,128)S(1)}, f32[32,128]{1,0:T(8,128)}, u32[]{:S(2)}) copy-start(f32[32,128]{1,0:T(8,128)} %get-tuple-element.13) | copy-start | bytes 49156

commit v6 on v5

--- a/solution.py
+++ b/solution.py
@@ -20,7 +20,7 @@
 INNER = 6144
 SEGS = 7168
 SHOWN = 8
-CHUNKS = 80
+CHUNKS = 48
 PANEL = 32
 PITCH = 40
 FOUR = 4
@@ -110,10 +110,10 @@
 
 
 def setup_kernel(
-    ends, cond, mask, shown, arrived, inverse, degree_out, table, rank, degree, sums, packed, counts, old_rows, turned_rows, small, counts_smem, sem
+    ends, cond, mask, shown, arrived, inverse, degree_out, table, rank, degree, near, sums, counts, old_rows, turned_rows, small, counts_smem, sem
 ):
     degree[...] = jnp.zeros_like(degree)
-    sums[...] = jnp.zeros_like(sums)
+    near[...] = jnp.zeros_like(near)
     width = 256
     before = lax.broadcasted_iota(I32, (width, width), 0) < lax.broadcasted_iota(I32, (width, width), 1)
     before = jnp.where(before, 1.0, 0.0).astype(BF16)
@@ -127,7 +127,7 @@
         degree[...] += dot_nt(jnp.concatenate(stacks, axis=1), jnp.concatenate(lanes, axis=1))
 
     def scan(step, carry):
-        nodes, values = [], []
+        nodes, values, stacks, lanes = [], [], [], []
         for i in range(SCANS):
             cols = pl.ds(pl.multiple_of((SCANS * step + i) * width, width), width)
             head = ends[0:1, cols]
@@ -138,9 +138,16 @@
             bucket = jnp.where((head >> 7) == (tail >> 7), head >> 7, -1)
             member = one_hot_rows(bucket, BLOCKS)
             ahead = dot_nn(spread(member, 1.0), before)
-            rank[:, cols] = jnp.sum(jnp.where(member, ahead + carry, 0.0), axis=0, keepdims=True)
+            place = jnp.sum(jnp.where(member, ahead + carry, 0.0), axis=0, keepdims=True)
+            rank[:, cols] = place
             carry = carry + jnp.sum(jnp.where(member, 1.0, 0.0), axis=1, keepdims=True)
+            order = place.astype(I32)
+            at_block = one_hot_rows(jnp.where(order < TILE, bucket, -1), BLOCKS)
+            fields = ((head & 127).astype(F32), (tail & 127).astype(F32)) + parts2(value)
+            stacks.append(jnp.concatenate([spread(at_block, field) for field in fields], axis=0))
+            lanes.append(one_hot_lanes(order & 127, TILE))
         add_degree(nodes, values)
+        near[...] += dot_nt(jnp.concatenate(stacks, axis=1), jnp.concatenate(lanes, axis=1))
         return carry
 
     total = lax.fori_loop(0, INNER // width // SCANS, scan, jnp.zeros((BLOCKS, 1), F32))
@@ -152,7 +159,7 @@
     deg = deg + (leak_rate + inflow_weight * mask[...].astype(F32))
     degree_out[...] = deg
 
-    chunks = jnp.floor((jnp.broadcast_to(total, (BLOCKS, TILE)) + 127.0) * (1.0 / 128.0))
+    chunks = jnp.maximum(jnp.floor((jnp.broadcast_to(total, (BLOCKS, TILE)) - 1.0) * (1.0 / 128.0)), 0.0)
     below = lax.broadcasted_iota(I32, (BLOCKS, BLOCKS), 1) < lax.broadcasted_iota(I32, (BLOCKS, BLOCKS), 0)
     start = dot_nn(jnp.where(below, 1.0, 0.0).astype(BF16), chunks.astype(BF16))
     counts[0:32, :] = start.astype(I32)
@@ -171,7 +178,7 @@
         bucket = jnp.where(inside, head >> 7, -1)
         base = jnp.sum(jnp.where(one_hot_rows(bucket, BLOCKS), start_column, 0.0), axis=0, keepdims=True)
         order = rank[:, cols].astype(I32)
-        chunk = jnp.where(inside, base.astype(I32) + (order >> 7), -1)
+        chunk = jnp.where(inside & (order >= TILE), base.astype(I32) + (order >> 7) - 1, -1)
         at_chunk = one_hot_rows(chunk, CHUNKS)
         values = ((head & 127).astype(F32), (tail & 127).astype(F32)) + parts2(cond[:, cols])
         stack = jnp.concatenate([spread(at_chunk, value) for value in values], axis=0)
@@ -179,22 +186,18 @@
         sums[...] += dot_nt(stack, lanes)
         return carry
 
-    lax.fori_loop(0, INNER // wide, compact, 0)
-    packed[...] = sums[...]
-    to_scalar.wait()
-
     row_id = lax.broadcasted_iota(I32, (TILE, TILE), 0)
     lane_id = lax.broadcasted_iota(I32, (TILE, TILE), 1)
 
-    def chunk_of(row, live):
-        head = packed[pl.ds(row, 1), :].astype(I32)
-        tail = packed[pl.ds(row + CHUNKS, 1), :].astype(I32)
+    def chunk_of(source, row, pitch):
+        head = source[pl.ds(row, 1), :].astype(I32)
+        tail = source[pl.ds(row + pitch, 1), :].astype(I32)
         at_head = row_id == head
         at_tail = row_id == tail
         left = jnp.concatenate([spread(at_head, 1.0), spread(at_tail, 1.0)], axis=1)
         right = []
         for k in range(2):
-            value = packed[pl.ds(row + (2 + k) * CHUNKS, 1), :] * live
+            value = source[pl.ds(row + (2 + k) * pitch, 1), :]
             right.append(jnp.concatenate([spread(at_tail, value), spread(at_head, value)], axis=1))
         both = dot_nt(left, jnp.concatenate(right, axis=0))
         return both[:, 0:TILE] + both[:, TILE:]
@@ -203,27 +206,29 @@
         filled = []
         for i in range(FILLS):
             block = step * FILLS + i
-            live = jnp.where(counts_smem[block + BLOCKS, 0] > 0, 1.0, 0.0)
-            off = chunk_of(counts_smem[block, 0], live)
+            off = chunk_of(near, block, BLOCKS)
             filled.append(jnp.where(row_id == lane_id, degree_out[pl.ds(block, 1), :], -off))
         for i in range(FILLS):
             table[pl.ds(pl.multiple_of((step * FILLS + i) * TILE, TILE), TILE), :] = filled[i]
         return carry
 
     lax.fori_loop(0, BLOCKS // FILLS, fill, 0)
+    to_scalar.wait()
 
     def refill(block, carry):
         rows = pl.ds(pl.multiple_of(block * TILE, TILE), TILE)
 
         def more(index, inner):
-            table[rows, :] = table[rows, :] - chunk_of(counts_smem[block, 0] + index, 1.0)
+            table[rows, :] = table[rows, :] - chunk_of(sums, counts_smem[block, 0] + index, CHUNKS)
             return inner
 
-        lax.fori_loop(1, counts_smem[block + BLOCKS, 0], more, 0)
+        lax.fori_loop(0, counts_smem[block + BLOCKS, 0], more, 0)
         return carry
 
-    @pl.when(counts_smem[64, 0] > 1)
+    @pl.when(counts_smem[64, 0] > 0)
     def _():
+        sums[...] = jnp.zeros_like(sums)
+        lax.fori_loop(0, INNER // wide, compact, 0)
         lax.fori_loop(0, BLOCKS, refill, 0)
 
     panel_lane = lax.broadcasted_iota(I32, (PANEL, TILE), 1)
@@ -554,7 +559,7 @@
             pltpu.VMEM((NODES, TILE), F32),
             pltpu.VMEM((1, INNER), F32),
             pltpu.VMEM((64, TILE), F32),
-            pltpu.VMEM((4 * CHUNKS, TILE), F32),
+            pltpu.VMEM((4 * BLOCKS, TILE), F32),
             pltpu.VMEM((4 * CHUNKS, TILE), F32),
             pltpu.VMEM((72, TILE), I32),
             pltpu.VMEM((BLOCKS * PITCH, TILE), F32),

time: 67.7 us -> 65.9 us (0.973)
  Pallas kernels: 63.7 us -> 61.9 us
    pallas_call x1, Pallas kernels: 20.7 us -> 18.8 us  [setup_call(): pl.pallas_call(setup_kernel, out_shape=(jax.ShapeDtypeStruct((BLOCKS, TIL...]
where the time goes in v6:
time: 65.9 us; the launch traced here: 65.4 us
  Pallas kernels  61.9 us (94%)
  local copies, waits for them, and re-layouts  2.18 us (3%)
  between operations  1.31 us (2%)
    pallas_call x1, Pallas kernels, per_device(): pl.pallas_call(functools.partial(solve_kernel, sizes), out_shape=(jax.Sha...  31.6 us
    pallas_call x1, Pallas kernels, setup_call(): pl.pallas_call(setup_kernel, out_shape=(jax.ShapeDtypeStruct((BLOCKS, TIL...  18.8 us
    pallas_call x1, Pallas kernels, per_device(): pl.pallas_call(functools.partial(head_kernel, parts), out_shape=(jax.Shap...  11.5 us
    unnamed x4, local copies, waits for them, and re-layouts  2.18 us

profile of v6, /device:TPU:1, one launch (start us, length us, event | category | flops | bytes accessed | tf_op | source)
XLA Modules:
  0.0 65.4 jit_solution(8800623259907626522)
XLA Ops:
  1.3 11.5 %conductances.1 = (f32[1,7168]{1,0:T(1,128)}, f32[8,128]{1,0:T(8,128)}) custom-call(s32[2,7168]{1,0:T(2,128)} %ends.5, f32[1,7168]{1,0:T(1,128)} %bitcast.6, f32[1,7168]{1,0:T(1,128)} %bitcast.7, s32[1]{0:T(128)S(6)} %copy.11.live), custom_call_target="tpu_custom_call" | custom-call | tf_op jit(solution)/shard_map/conductances/pallas_call | solution.py:579
  12.8 18.8 %inverses.1 = (bf16[32,128,128]{2,1,0:T(8,128)(2,1)}, f32[32,128]{1,0:T(8,128)}) custom-call(s32[2,7168]{1,0:T(2,128)} %ends.5, f32[1,7168]{1,0:T(1,128)} %get-tuple-element.8.cond, s32[32,128]{1,0:T(8,128)} %bitcast.4, s32[8]{0:T(128)} %shown.3, f32[8,128]{1,0:T(8,128)} %get-tuple-element.9.arrived), custom_call_target="tpu_custom_call" | custom-call | tf_op jit(solution)/shard_map/inverses/pallas_call | solution.py:553
  31.6 31.6 %gradients.1 = (f32[8,4096]{1,0:T(8,128)}, f32[32,128]{1,0:T(8,128)}) custom-call(f32[8,4096]{1,0:T(8,128)} %inflow.1, s32[32,128]{1,0:T(8,128)} %bitcast.5, s32[2,7168]{1,0:T(2,128)} %ends.5, f32[1,7168]{1,0:T(1,128)} %get-tuple-element.8.cond, f32[32,128]{1,0:T(8,128)} %get-tuple-element.10.degree, bf16[32,128,128]{2,1,0:T(8,128)(2,1)} %get-tuple-element.11.inverse, ...), custom_call_target="tpu_custom_call" | custom-call | tf_op jit(solution)/shard_map/gradients/pallas_call | solution.py:591
  63.2 0.0 copy-start
  63.2 1.6 %copy.12 = f32[8,4096]{1,0:T(8,128)} copy(f32[8,4096]{1,0:T(8,128)} %get-tuple-element.16) | data formatting | bytes 262144
  64.8 0.0 copy-done
  64.8 0.6 copy.13
Async XLA Ops:
  63.2 1.6 %copy-start = (f32[32,128]{1,0:T(8,128)S(1)}, f32[32,128]{1,0:T(8,128)}, u32[]{:S(2)}) copy-start(f32[32,128]{1,0:T(8,128)} %get-tuple-element.13) | copy-start | bytes 49156

commit v7 on v6

--- a/solution.py
+++ b/solution.py
@@ -24,7 +24,7 @@
 PANEL = 32
 PITCH = 40
 FOUR = 4
-UNROLL = 8
+UNROLL = 12
 SCANS = 4
 FILLS = 8
 
@@ -313,12 +313,12 @@
     upper = lax.rem(place + 1, parts)
     lower = lax.rem(place + parts - 1, parts)
     core = lax.rem(place, 2)
-    column = lax.rem(place // 2, depth_z)
-    line = place // (2 * depth_z)
+    column = lax.rem(lax.div(place, 2), depth_z)
+    line = lax.div(place, 2 * depth_z)
     seat = line * 2 + core
 
     def plane_place(other):
-        return ((other // 2) * depth_z + column) * 2 + lax.rem(other, 2)
+        return (lax.div(other, 2) * depth_z + column) * 2 + lax.rem(other, 2)
 
     def column_place(other):
         return (line * depth_z + other) * 2 + core

time: 65.9 us -> 65.2 us (0.989)
    pallas_call x1, Pallas kernels: 31.6 us -> 30.9 us  [per_device(): pl.pallas_call(functools.partial(solve_kernel, sizes), out_shape=(jax.Sha...]
where the time goes in v7:
time: 65.2 us; the launch traced here: 64.8 us
  Pallas kernels  61.3 us (94%)
  local copies, waits for them, and re-layouts  2.18 us (3%)
  between operations  1.31 us (2%)
    pallas_call x1, Pallas kernels, per_device(): pl.pallas_call(functools.partial(solve_kernel, sizes), out_shape=(jax.Sha...  30.9 us
    pallas_call x1, Pallas kernels, setup_call(): pl.pallas_call(setup_kernel, out_shape=(jax.ShapeDtypeStruct((BLOCKS, TIL...  18.8 us
    pallas_call x1, Pallas kernels, per_device(): pl.pallas_call(functools.partial(head_kernel, parts), out_shape=(jax.Shap...  11.5 us
    unnamed x4, local copies, waits for them, and re-layouts  2.18 us

profile of v7, /device:TPU:1, one launch (start us, length us, event | category | flops | bytes accessed | tf_op | source)
XLA Modules:
  0.0 64.8 jit_solution(592716258201381461)
XLA Ops:
  1.3 11.5 %conductances.1 = (f32[1,7168]{1,0:T(1,128)}, f32[8,128]{1,0:T(8,128)}) custom-call(s32[2,7168]{1,0:T(2,128)} %ends.5, f32[1,7168]{1,0:T(1,128)} %bitcast.6, f32[1,7168]{1,0:T(1,128)} %bitcast.7, s32[1]{0:T(128)S(6)} %copy.11.live), custom_call_target="tpu_custom_call" | custom-call | tf_op jit(solution)/shard_map/conductances/pallas_call | solution.py:579
  12.8 18.8 %inverses.1 = (bf16[32,128,128]{2,1,0:T(8,128)(2,1)}, f32[32,128]{1,0:T(8,128)}) custom-call(s32[2,7168]{1,0:T(2,128)} %ends.5, f32[1,7168]{1,0:T(1,128)} %get-tuple-element.8.cond, s32[32,128]{1,0:T(8,128)} %bitcast.4, s32[8]{0:T(128)} %shown.3, f32[8,128]{1,0:T(8,128)} %get-tuple-element.9.arrived), custom_call_target="tpu_custom_call" | custom-call | tf_op jit(solution)/shard_map/inverses/pallas_call | solution.py:553
  31.6 30.9 %gradients.1 = (f32[8,4096]{1,0:T(8,128)}, f32[32,128]{1,0:T(8,128)}) custom-call(f32[8,4096]{1,0:T(8,128)} %inflow.1, s32[32,128]{1,0:T(8,128)} %bitcast.5, s32[2,7168]{1,0:T(2,128)} %ends.5, f32[1,7168]{1,0:T(1,128)} %get-tuple-element.8.cond, f32[32,128]{1,0:T(8,128)} %get-tuple-element.10.degree, bf16[32,128,128]{2,1,0:T(8,128)(2,1)} %get-tuple-element.11.inverse, ...), custom_call_target="tpu_custom_call" | custom-call | tf_op jit(solution)/shard_map/gradients/pallas_call | solution.py:591
  62.6 0.0 copy-start
  62.6 1.6 %copy.12 = f32[8,4096]{1,0:T(8,128)} copy(f32[8,4096]{1,0:T(8,128)} %get-tuple-element.16) | data formatting | bytes 262144
  64.1 0.0 copy-done
  64.1 0.6 copy.13
Async XLA Ops:
  62.6 1.6 %copy-start = (f32[32,128]{1,0:T(8,128)S(1)}, f32[32,128]{1,0:T(8,128)}, u32[]{:S(2)}) copy-start(f32[32,128]{1,0:T(8,128)} %get-tuple-element.13) | copy-start | bytes 49156
